TPU v7x, 256 devices: a whole 4x4x8 slice. The times are simulated.
256 devices in a mesh: req: 32 (over y, x, core), tp: 8 (over z).
Axes of the slice: x: 4, y: 4, z: 8, core: 2. Of those that a mesh axis runs over, the one named last changes fastest.
Arguments:
- tokens: bfloat16 [32, 768, 2048], P('req', None, 'tp'), may hold values from -6 to 6
- q_weight: bfloat16 [2048, 2048], P(None, 'tp'), may hold values from -0.125 to 0.125
- k_weight: bfloat16 [2048, 2048], P(None, 'tp'), may hold values from -0.125 to 0.125
- v_weight: bfloat16 [2048, 2048], P(None, 'tp'), may hold values from -0.125 to 0.125
- o_weight: bfloat16 [2048, 2048], P('tp'), may hold values from -0.125 to 0.125
- q_gain: bfloat16 [2048], P('tp'), may hold values from 0.099609375 to 1.8984375
- k_gain: bfloat16 [2048], P('tp'), may hold values from 0.099609375 to 1.8984375
- post_gain: bfloat16 [2048], P('tp'), may hold values from 0.099609375 to 1.8984375
- key_pool: bfloat16 [1024, 128, 2048], P('req', None, 'tp'), may hold values from -400 to 400
- value_pool: bfloat16 [1024, 128, 2048], P('req', None, 'tp'), may hold values from -6 to 6
- cache_len: int32 [32], replicated, may hold values from 1 to 4096, as said below
- page_table: int32 [32, 32], replicated, may hold values from -1 to 1023, as said below
Outputs:
- mixed: bfloat16 [32, 768, 2048], P('req', None, 'tp')
- new_keys: bfloat16 [32, 768, 2048], P('req', None, 'tp')
- new_values: bfloat16 [32, 768, 2048], P('req', None, 'tp')
Inputs may be any that keep to these rules, and one draw needn't show every extreme that they name: `cache_len`: on some index of req the one request hold 4096 cached tokens. `page_table`: entry p of request r is a pool page (index d * 32 + local page of index d of req) for p < ceil(cache_len[r] / 128) and -1 otherwise; no pool page is named twice; the pages named by the requests of one index of req lie at most 1 on any one index of req, and some pair of indices reaches 1.
All inputs are finite; a program needn't handle non-finite values.
Results may differ from a plain program's by a relative error of at most 0.013.
Values may be sent and summed in bfloat16 or wider, within the bound.
No kernel may reach another device: no remote copies, remote signals or barrier semaphores. Data moves between devices by JAX's collectives and lax.ppermute only.
A program may use at most 64 MiB of HBM per device.

v0:
```python
import functools

import jax
import jax.numpy as jnp
from jax import lax
from jax.experimental import pallas as pl
from jax.experimental.pallas import tpu as pltpu
from jax.sharding import PartitionSpec as P


HEAD_DIM = 128
EPSILON = 1e-06
ROPE_BASE = 500000.0
NEG = -1e30
F32 = jnp.float32
BF16 = jnp.bfloat16
VMEM_SPEC = pl.BlockSpec(memory_space=pltpu.VMEM)
SMEM_SPEC = pl.BlockSpec(memory_space=pltpu.SMEM)
HBM_SPEC = pl.BlockSpec(memory_space=pltpu.HBM)


def cost(flops, moved):
    return pl.CostEstimate(flops=flops, bytes_accessed=moved, transcendentals=0)


def params(mib):
    return pltpu.CompilerParams(vmem_limit_bytes=mib << 20)


def pick_kernel(
    chosen, place, lengths, freqs, key_pool, value_pool, out, cosine, sine, held, sem
):
    slots, page = out.shape[0], key_pool.shape[1]
    group = 8
    for slot in range(slots):
        index = chosen[slot]
        for part, pool in enumerate((key_pool, value_pool)):
            pltpu.make_async_copy(
                pool.at[index], held.at[slot, pl.ds(part * page, page)], sem.at[0, slot // group]
            ).start()

    length = lengths[place[0]]
    rows = cosine.shape[0]
    tile = 256
    for start in range(0, rows, tile):
        row = lax.broadcasted_iota(jnp.int32, (tile, 128), 0)
        lane = lax.broadcasted_iota(jnp.int32, (tile, 128), 1)
        angles = (row + (length + start)).astype(F32) * freqs[...]
        cosine[start : start + tile, :] = jnp.cos(angles)
        turned = jnp.sin(angles)
        sine[start : start + tile, :] = jnp.where(lane < 64, -turned, turned)

    leaving = []
    for at in range(0, slots, group):
        here = pl.ds(at, group)
        pltpu.make_async_copy(out.at[here], held.at[here], sem.at[0, at // group]).wait()
        leaving.append(pltpu.make_async_copy(held.at[here], out.at[here], sem.at[1, at // group]))
        leaving[-1].start()
    for copy in leaving:
        copy.wait()


def pick_pages(rows, chosen, place, lengths, freqs, key_pool, value_pool):
    slots = chosen.shape[0]
    _, page, width = key_pool.shape
    return pl.pallas_call(
        pick_kernel,
        out_shape=(
            jax.ShapeDtypeStruct((slots, 2 * page, width), BF16),
            jax.ShapeDtypeStruct((rows, HEAD_DIM), F32),
            jax.ShapeDtypeStruct((rows, HEAD_DIM), F32),
        ),
        in_specs=[SMEM_SPEC] * 3 + [VMEM_SPEC, HBM_SPEC, HBM_SPEC],
        out_specs=(HBM_SPEC, VMEM_SPEC, VMEM_SPEC),
        scratch_shapes=[
            pltpu.VMEM((slots, 2 * page, width), BF16),
            pltpu.SemaphoreType.DMA((2, slots // 8)),
        ],
        compiler_params=params(62),
        name="pick_pages",
    )(chosen, place, lengths, freqs, key_pool, value_pool)


def row_sums(values):
    squares = values * values
    folded = squares[:, :128]
    for start in range(128, values.shape[1], 128):
        folded = folded + squares[:, start : start + 128]
    return jnp.sum(folded.T, axis=0, keepdims=True)


def qkv_kernel(count, parts, order, *refs):
    blocks = refs[: count * parts]
    wq, wk, wv, q_out, k_out, v_out, stat, x, w, sem, w_sem = refs[count * parts :]
    depth = x.shape[2]
    rows = x.shape[1]
    piece = rows // parts

    def weight_copy(which, source):
        return pltpu.make_async_copy(source, w.at[which], w_sem.at[which])

    def block_copy(at, part):
        return pltpu.make_async_copy(
            blocks[at * parts + part], x.at[at, pl.ds(part * piece, piece)], sem.at[at, part]
        )

    weight_copy(0, wq).start()
    for at in range(count):
        block_copy(at, 0).start()
    weight_copy(1, wk).start()
    weight_copy(2, wv).start()
    for part in range(1, parts):
        for at in range(count):
            block_copy(at, part).start()
    tile = 256
    ready = 0
    for start in range(0, rows, tile):
        here = slice(start, start + tile)
        needed = -(-(start + tile) // piece)
        for which, (source, out) in enumerate(((wq, q_out), (wk, k_out), (wv, v_out))):
            if start == 0:
                weight_copy(which, source).wait()
            total = None
            for at in range(count):
                for part in range(ready, needed):
                    block_copy(at, part).wait()
                span = pl.ds(pl.multiple_of(order[at] * depth, depth), depth)
                term = jnp.dot(x[at, here, :], w[which, span, :], preferred_element_type=F32)
                total = term if total is None else total + term
            ready = needed
            out[here, :] = total.astype(out.dtype)
            if which < 2:
                stat[which : which + 1, here] = row_sums(total)


def qkv(order, blocks, wq, wk, wv):
    count = len(blocks)
    parts = len(blocks[0])
    piece, depth = blocks[0][0].shape
    rows = piece * parts
    columns = wq.shape[1]
    return pl.pallas_call(
        functools.partial(qkv_kernel, count, parts),
        out_shape=(
            jax.ShapeDtypeStruct((rows, columns), F32),
            jax.ShapeDtypeStruct((rows, columns), F32),
            jax.ShapeDtypeStruct((rows, columns), BF16),
            jax.ShapeDtypeStruct((2, rows), F32),
        ),
        in_specs=[SMEM_SPEC] + [HBM_SPEC] * (count * parts + 3),
        out_specs=(VMEM_SPEC,) * 4,
        scratch_shapes=[
            pltpu.VMEM((count, rows, depth), BF16),
            pltpu.VMEM((3, wq.shape[0], columns), BF16),
            pltpu.SemaphoreType.DMA((count, parts)),
            pltpu.SemaphoreType.DMA((3,)),
        ],
        compiler_params=params(62),
        cost_estimate=cost(2 * rows * depth * count * 3 * columns, 9 << 20),
        name="qkv",
    )(order, *[piece for block in blocks for piece in block], wq, wk, wv)


def down_rows(line):
    return jnp.broadcast_to(line, (128, line.shape[1])).T


def attend_kernel(
    full,
    place,
    lengths,
    page_table,
    stat,
    q_gain,
    k_gain,
    q_hbm,
    k_hbm,
    v_hbm,
    cos_hbm,
    sin_hbm,
    pages_hbm,
    out,
    keys_out,
    raw,
    table,
    query,
    new_k,
    new_v,
    pages,
    ones,
    scores,
    counts,
    sem,
    page_sem,
):
    tile = 256
    slots = pages.shape[0]
    rows, columns = query.shape
    page = pages.shape[1] // 2
    group = 8
    span = group * page
    cached = slots * page
    factor = HEAD_DIM**-0.5 * 1.4426950408889634
    contract = (((1,), (1,)), ((), ()))
    small = [
        pltpu.make_async_copy(source, held, sem.at[at])
        for at, (source, held) in enumerate(
            (
                (q_hbm, raw.at[0]),
                (cos_hbm, table.at[0]),
                (sin_hbm, table.at[1]),
                (k_hbm, raw.at[1]),
                (v_hbm, new_v),
            )
        )
    ]
    for copy in small:
        copy.start()
    parts = [
        pltpu.make_async_copy(
            pages_hbm.at[pl.ds(at, group)], pages.at[pl.ds(at, group)], page_sem.at[at // group]
        )
        for at in range(0, slots, group)
    ]
    for copy in parts:
        copy.start()

    owner = place[0]
    length = lengths[owner]
    ones[...] = jnp.ones(ones.shape, BF16)

    @pl.loop(0, slots)
    def _(slot):
        counts[slot] = 0

    @pl.loop(0, page_table.shape[1])
    def _(at):
        entry = page_table[owner, at]

        @pl.when(entry >= 0)
        def _():
            counts[lax.div(entry, slots)] = length - at * page

    for which, gain in enumerate((q_gain, k_gain)):
        for copy in small[:3] if which == 0 else small[3:4]:
            copy.wait()
        for start in range(0, rows, tile):
            here = slice(start, start + tile)
            scale = lax.rsqrt(down_rows(stat[which : which + 1, here]) / full + EPSILON)
            for low in range(0, columns, HEAD_DIM):
                lanes = slice(low, low + HEAD_DIM)
                value = raw[which, here, lanes] * scale * gain[0:1, lanes].astype(F32)
                turned = value * table[0, here, :]
                turned = turned + pltpu.roll(value, HEAD_DIM // 2, 1) * table[1, here, :]
                turned = turned.astype(BF16)
                if which == 0:
                    query[here, lanes] = turned
                else:
                    new_k[here, lanes] = turned
                    keys_out[here, lanes] = turned
    small[4].wait()
    for copy in parts:
        copy.wait()

    first = lax.div(page_table[owner, 0], slots)
    key = jnp.broadcast_to(pages[first, 0:1, :], (page, columns))

    @pl.loop(0, slots)
    def _(slot):
        exist = counts[slot]

        @pl.when(exist < page)
        def _():
            for low in range(0, columns, 128):
                lanes = slice(low, low + 128)
                row = lax.broadcasted_iota(jnp.int32, (page, 128), 0)
                keep = row < exist
                kept = pages[slot, :page, lanes].astype(F32)
                spare = key[:, lanes].astype(F32)
                pages[slot, :page, lanes] = jnp.where(keep, kept, spare).astype(BF16)
                value = pages[slot, page:, lanes].astype(F32)
                pages[slot, page:, lanes] = jnp.where(keep, value, 0.0).astype(BF16)
                if low == 0:
                    ones[slot] = jnp.where(keep, 1.0, 0.0).astype(BF16)

    one = jnp.ones((tile, HEAD_DIM), BF16)
    for column in range(0, columns, HEAD_DIM):
        head = slice(column, column + HEAD_DIM)
        for start in range(0, rows, tile):
            q = query[start : start + tile, head]
            fresh = start + tile
            top = None
            for at in range(0, slots, group):
                k = pages[at : at + group, :page, head].reshape(span, HEAD_DIM)
                s = lax.dot_general(q, k, contract, preferred_element_type=F32)
                scores[:, at * page : at * page + span] = s
                for lane in range(0, span, 128):
                    part = s[:, lane : lane + 128]
                    top = part if top is None else jnp.maximum(top, part)
            for low in range(0, fresh, tile):
                k = new_k[low : low + tile, head]
                s = lax.dot_general(q, k, contract, preferred_element_type=F32)
                if low == start:
                    row = lax.broadcasted_iota(jnp.int32, s.shape, 0)
                    col = lax.broadcasted_iota(jnp.int32, s.shape, 1)
                    s = jnp.where(row >= col, s, NEG)
                scores[:, cached + low : cached + low + tile] = s
                for lane in range(0, tile, 128):
                    top = jnp.maximum(top, s[:, lane : lane + 128])
            peak = jnp.max(top, axis=1, keepdims=True)
            result = None
            for at in range(0, slots, group):
                raised = jnp.exp2((scores[:, at * page : at * page + span] - peak) * factor)
                v = jnp.concatenate(
                    [
                        pages[at : at + group, page:, head].reshape(span, HEAD_DIM),
                        ones[at : at + group].reshape(span, HEAD_DIM),
                    ],
                    1,
                )
                term = jnp.dot(raised.astype(BF16), v, preferred_element_type=F32)
                result = term if result is None else result + term
            for low in range(0, fresh, tile):
                raised = jnp.exp2(
                    (scores[:, cached + low : cached + low + tile] - peak) * factor
                )
                v = jnp.concatenate([new_v[low : low + tile, head], one], 1)
                result = result + jnp.dot(raised.astype(BF16), v, preferred_element_type=F32)
            result = result[:, :HEAD_DIM] / result[:, HEAD_DIM:]
            out[start : start + tile, head] = result.astype(BF16)


def attend(
    full, place, lengths, page_table, stat, q_gain, k_gain, q_proj, k_proj, new_v, cosine, sine, pages
):
    rows, columns = q_proj.shape
    slots, both, _ = pages.shape
    keys = slots * both // 2 + rows
    held = pltpu.VMEM((rows, columns), BF16)
    shape = jax.ShapeDtypeStruct((rows, columns), BF16)
    return pl.pallas_call(
        functools.partial(attend_kernel, full),
        out_shape=(shape, shape),
        in_specs=[SMEM_SPEC] * 3 + [VMEM_SPEC] * 3 + [HBM_SPEC] * 6,
        out_specs=(VMEM_SPEC, VMEM_SPEC),
        scratch_shapes=[
            pltpu.VMEM((2, rows, columns), F32),
            pltpu.VMEM((2, rows, HEAD_DIM), F32),
            held,
            held,
            held,
            pltpu.VMEM((slots, both, columns), BF16),
            pltpu.VMEM((slots, both // 2, HEAD_DIM), BF16),
            pltpu.VMEM((256, keys), F32),
            pltpu.SMEM((slots,), jnp.int32),
            pltpu.SemaphoreType.DMA((5,)),
            pltpu.SemaphoreType.DMA((slots,)),
        ],
        compiler_params=params(62),
        cost_estimate=cost(4 * rows * keys * columns, 9 << 20),
        name="attend",
    )(place, lengths, page_table, stat, q_gain, k_gain, q_proj, k_proj, new_v, cosine, sine, pages)


def project_kernel(full, order, *refs):
    heads, *blocks, near_half, far_half, out, held, weight, total, sem = refs
    count = len(blocks) + 1
    depth = heads.shape[1]
    share = total.shape[0]
    half = depth // 2
    core = order[count]
    copies = [
        pltpu.make_async_copy(block, weight.at[at], sem.at[at]) for at, block in enumerate(blocks)
    ]
    for at, (source, offset) in enumerate(((near_half, core), (far_half, 1 - core))):
        rows = pl.ds(pl.multiple_of(offset * half, half), half)
        copies.append(
            pltpu.make_async_copy(source, weight.at[count - 1, rows], sem.at[count - 1 + at])
        )
    load = pltpu.make_async_copy(heads, held, sem.at[count + 1])
    load.start()
    for copy in copies:
        copy.start()
    load.wait()
    wide = 1024
    for at in range(count):
        copies[at].wait()
        if at == count - 1:
            copies[count].wait()
        rows = pl.ds(pl.multiple_of(order[at] * share, share), share)
        x = held[rows, :]
        for start in range(0, full, wide):
            span = slice(start, start + wide)
            term = jnp.dot(x, weight[at, :, span], preferred_element_type=F32)
            total[:, span] = term if at == 0 else total[:, span] + term
    value = total[...]
    scale = lax.rsqrt(jnp.sum(value * value, axis=1, keepdims=True) / full + EPSILON)
    for at in range(count):
        normed = total[:, at * depth : (at + 1) * depth] * scale
        out[at * share : (at + 1) * share, :] = normed.astype(BF16)


def project(order, heads, blocks, near_half, far_half):
    rows, depth = heads.shape
    count = len(blocks) + 1
    full = blocks[0].shape[1]
    share = rows // count
    return pl.pallas_call(
        functools.partial(project_kernel, full),
        out_shape=jax.ShapeDtypeStruct((rows, depth), BF16),
        in_specs=[SMEM_SPEC] + [HBM_SPEC] * (count + 2),
        out_specs=VMEM_SPEC,
        scratch_shapes=[
            pltpu.VMEM((rows, depth), BF16),
            pltpu.VMEM((count, depth, full), BF16),
            pltpu.VMEM((share, full), F32),
            pltpu.SemaphoreType.DMA((count + 2,)),
        ],
        compiler_params=params(62),
        cost_estimate=cost(2 * rows * depth * full, 9 << 20),
        name="project",
    )(order, heads, *blocks, near_half, far_half)


def ring_gather(block, size, parts):
    right = [(i, (i + 1) % size) for i in range(size)]
    left = [(i, (i - 1) % size) for i in range(size)]
    piece = block.shape[0] // parts
    pieces = [block[at * piece : (at + 1) * piece] for at in range(parts)]
    found = [pieces]
    forward, backward = list(pieces), list(pieces)
    for _ in range((size - 1) // 2):
        for at in range(parts):
            forward[at] = lax.ppermute(forward[at], "tp", right)
            backward[at] = lax.ppermute(backward[at], "tp", left)
        found += [list(forward), list(backward)]
    far = [
        lax.ppermute(forward[at], "tp", right)
        if at < parts // 2
        else lax.ppermute(backward[at], "tp", left)
        for at in range(parts)
    ]
    return found + [far]


def ring_order(size):
    me = lax.axis_index("tp")
    steps = [0]
    for step in range(1, (size - 1) // 2 + 1):
        steps += [-step, step]
    steps.append(size // 2)
    return (me + jnp.array(steps, jnp.int32) + size) % size


def weight_moves(owners, size):
    onward = []
    swap = []
    for r in range(owners):
        for t in range(size):
            to = (t + (1 if r % 2 == 0 else -1)) % size
            onward.append((r * size + t, r * size + to))
            swap.append((r * size + t, (r ^ 1) * size + t))
    return onward, swap


def after(value, *others):
    return lax.optimization_barrier((value, *others))[0]


def body(
    tokens,
    q_weight,
    k_weight,
    v_weight,
    o_weight,
    q_gain,
    k_gain,
    post_gain,
    key_pool,
    value_pool,
    cache_len,
    page_table,
):
    _, block_len, feature_part = tokens.shape
    columns = q_weight.shape[1]
    owner = lax.axis_index("req")
    owners = lax.axis_size("req")
    size = lax.axis_size("tp")
    full = columns * size
    flat = tokens.reshape(block_len, feature_part)
    pool_dev, _, _ = key_pool.shape

    valid = page_table >= 0
    source = jnp.where(valid, page_table // pool_dev, -1)
    local = jnp.where(valid, page_table % pool_dev, 0)
    chosen = jnp.sum(jnp.where(source == owner, local, 0), 1)
    half = HEAD_DIM // 2
    freqs = jnp.power(jnp.float32(ROPE_BASE), -jnp.arange(half, dtype=F32) * 2.0 / HEAD_DIM)
    freqs = jnp.concatenate([freqs, freqs])[None]
    outgoing, cosine, sine = pick_pages(
        block_len, chosen, owner[None], cache_len, freqs, key_pool, value_pool
    )
    arrived = lax.all_to_all(outgoing, "req", split_axis=0, concat_axis=0, tiled=True)

    axes = ("req", "tp")
    onward, swap = weight_moves(owners, size)

    def move(value, pairs):
        return lax.ppermute(value, axes, pairs)

    order = ring_order(size)
    blocks = ring_gather(after(flat, outgoing), size, 2)
    o_1 = move(o_weight, onward)
    o_1 = after(o_1, *(piece for block in blocks[-3:] for piece in block))
    o_2 = move(o_1, onward)
    s_1 = move(o_1, swap)
    q_proj, k_proj, new_values, stat = qkv(order, blocks, q_weight, k_weight, v_weight)
    stat = lax.psum(stat, "tp")
    o_2 = after(o_2, stat)
    o_3 = move(o_2, onward)
    s_2 = move(o_2, swap)
    attended, new_keys = attend(
        full,
        owner[None],
        cache_len,
        page_table,
        stat,
        q_gain[None],
        k_gain[None],
        q_proj,
        k_proj,
        new_values,
        cosine,
        sine,
        arrived,
    )
    core = owner % 2
    share = o_weight.shape[0] // 2
    o_4 = move(lax.dynamic_slice_in_dim(o_3, core * share, share, 0), onward)
    s_3 = move(o_3, swap)
    s_4 = move(o_4, swap)
    heads = lax.all_to_all(attended, "tp", split_axis=0, concat_axis=0, tiled=True)

    me = lax.axis_index("tp")
    turn = 1 - 2 * core
    steps = [0]
    for step in range(1, (size - 1) // 2 + 1):
        steps += [-step, step]
    steps.append(size // 2)
    weight_order = (me + turn * jnp.array(steps, jnp.int32) + size) % size
    weight_order = jnp.concatenate([weight_order, core[None].astype(jnp.int32)])
    normed = project(
        weight_order, heads, [o_weight, o_1, s_1, o_2, s_2, o_3, s_3], o_4, s_4
    )
    normed = lax.all_to_all(normed, "tp", split_axis=0, concat_axis=0, tiled=True)
    mixed = flat.astype(F32) + normed.astype(F32) * post_gain.astype(F32)
    return (mixed.astype(BF16)[None], new_keys[None], new_values[None])


def solution(mesh):
    placed = (
        P("req", None, "tp"),
        P(None, "tp"),
        P(None, "tp"),
        P(None, "tp"),
        P("tp", None),
        P("tp"),
        P("tp"),
        P("tp"),
        P("req", None, "tp"),
        P("req", None, "tp"),
        P(),
        P(),
    )

    return jax.shard_map(
        body,
        mesh=mesh,
        in_specs=placed,
        out_specs=(P("req", None, "tp"), P("req", None, "tp"), P("req", None, "tp")),
        check_vma=False,
    )
```

profile of v0, /device:TPU:1, one launch (start us, length us, event | category | flops | bytes accessed | tf_op | source)
XLA Modules:
  0.0 179.1 jit_solution(11919317782595672381)
XLA Ops:
  2.6 6.5 %pick_pages.1 = (bf16[32,256,256]{2,1,0:T(8,128)(2,1)}, f32[768,128]{1,0:T(8,128)}, f32[768,128]{1,0:T(8,128)}) custom-call(s32[32]{0:T(128)} %fusion.6.chosen, s32[1]{0:T(128)} %bitcast.1.place, s32[32]{0:T(128)} %lengths.3, f32[1,128]{1,0:T(1,128)} %maximum_bitcast_fusion.freqs, bf16[32,128,256]{2,1,0:T(8,128)(2,1)} %key_pool.1, ...), custom_call_target="tpu_custom_call" | custom-call | tf_op jit(solution)/shard_map/pick_pages/pallas_call | solution.py:66
  9.2 8.6 %all-to-all-start = ((bf16[32,256,256]{2,1,0:T(8,128)(2,1)}), bf16[32,256,256]{2,1,0:T(8,128)(2,1)}, u32[]{:S(2)}, u32[]{:S(2)}) async-start(bf16[32,256,256]{2,1,0:T(8,128)(2,1)} %get-tuple-element.15), calls=%async_computation | async-start | bytes 8388608 | tf_op jit(solution)/shard_map/all_to_all | solution.py:503
  17.8 5.7 %collective-permute-start.14 = (bf16[256,2048]{1,0:T(8,128)(2,1)S(1)}, bf16[256,2048]{1,0:T(8,128)(2,1)S(1)}, u32[]{:S(2)}, u32[]{:S(2)}) collective-permute-start(bf16[256,2048]{1,0:T(8,128)(2,1)S(1)} %copy-done.3), channel_id=1, source_target_pairs={{0,1},{1,2},{2,3},{3,4},{4,5},{5,6},{6,7},{7,0},{8,15},{9,8},{10,9... | collective-permute-start | bytes 3145736 | tf_op jit(solution)/shard_map/ppermute | solution.py:509
  25.1 2.7 %collective-permute-start.2 = (bf16[384,256]{1,0:T(8,128)(2,1)S(1)}, bf16[384,256]{1,0:T(8,128)(2,1)S(1)}, u32[]{:S(2)}, u32[]{:S(2)}) collective-permute-start(bf16[384,256]{1,0:T(8,128)(2,1)S(1)} %get-tuple-element.28.refs_0_), channel_id=1, source_target_pairs={{0,7},{1,0},{2,1},{3,2},{4,3},{5,4},{6,5},{7,6},{8,15},{9,8},{10,9... | collective-permute-start | bytes 589832 | tf_op jit(solution)/shard_map/ppermute | solution.py:435
  27.8 15.9 %collective-permute-done.3.refs_5_ = bf16[384,256]{1,0:T(8,128)(2,1)S(1)} collective-permute-done((bf16[384,256]{1,0:T(8,128)(2,1)S(1)}, bf16[384,256]{1,0:T(8,128)(2,1)S(1)}, u32[]{:S(2)}, u32[]{:S(2)}) %collective-permute-start.3) | collective-permute-done | bytes 196640 | tf_op jit(solution)/shard_map/ppermute | solution.py:435
  43.7 3.5 %collective-permute-start.7 = (bf16[384,256]{1,0:T(8,128)(2,1)S(1)}, bf16[384,256]{1,0:T(8,128)(2,1)S(1)}, u32[]{:S(2)}, u32[]{:S(2)}) collective-permute-start(bf16[384,256]{1,0:T(8,128)(2,1)S(1)} %collective-permute-done.3.refs_5_), channel_id=1, source_target_pairs={{0,7},{1,0},{2,1},{3,2},{4,3},{5,4},{6,5},{7,6},{8,15},{9,8},{10,9... | collective-permute-start | bytes 589832 | tf_op jit(solution)/shard_map/ppermute | solution.py:435
  47.3 2.6 %collective-permute-start.6 = (bf16[384,256]{1,0:T(8,128)(2,1)S(1)}, bf16[384,256]{1,0:T(8,128)(2,1)S(1)}, u32[]{:S(2)}, u32[]{:S(2)}) collective-permute-start(bf16[384,256]{1,0:T(8,128)(2,1)S(1)} %collective-permute-done.2.refs_4_), channel_id=1, source_target_pairs={{0,7},{1,0},{2,1},{3,2},{4,3},{5,4},{6,5},{7,6},{8,15},{9,8},{10,9... | collective-permute-start | bytes 589832 | tf_op jit(solution)/shard_map/ppermute | solution.py:435
  50.4 3.5 %collective-permute-start.11 = (bf16[384,256]{1,0:T(8,128)(2,1)S(1)}, bf16[384,256]{1,0:T(8,128)(2,1)S(1)}, u32[]{:S(2)}, u32[]{:S(2)}) collective-permute-start(bf16[384,256]{1,0:T(8,128)(2,1)S(1)} %collective-permute-done.7.refs_9_), channel_id=1, source_target_pairs={{0,7},{1,0},{2,1},{3,2},{4,3},{5,4},{6,5},{7,6},{8,15},{9,8},{10,9... | collective-permute-start | bytes 589832 | tf_op jit(solution)/shard_map/ppermute | solution.py:435
  54.0 3.6 %collective-permute-done.5.refs_7_ = bf16[384,256]{1,0:T(8,128)(2,1)S(1)} collective-permute-done((bf16[384,256]{1,0:T(8,128)(2,1)S(1)}, bf16[384,256]{1,0:T(8,128)(2,1)S(1)}, u32[]{:S(2)}, u32[]{:S(2)}) %collective-permute-start.5) | collective-permute-done | bytes 196640 | tf_op jit(solution)/shard_map/ppermute | solution.py:434
  57.7 2.7 %collective-permute-start.10 = (bf16[384,256]{1,0:T(8,128)(2,1)S(1)}, bf16[384,256]{1,0:T(8,128)(2,1)S(1)}, u32[]{:S(2)}, u32[]{:S(2)}) collective-permute-start(bf16[384,256]{1,0:T(8,128)(2,1)S(1)} %collective-permute-done.6.refs_8_), channel_id=1, source_target_pairs={{0,7},{1,0},{2,1},{3,2},{4,3},{5,4},{6,5},{7,6},{8,15},{9,8},{10,9... | collective-permute-start | bytes 589832 | tf_op jit(solution)/shard_map/ppermute | solution.py:435
  62.2 2.1 %collective-permute-done.9.refs_11_ = bf16[384,256]{1,0:T(8,128)(2,1)S(1)} collective-permute-done((bf16[384,256]{1,0:T(8,128)(2,1)S(1)}, bf16[384,256]{1,0:T(8,128)(2,1)S(1)}, u32[]{:S(2)}, u32[]{:S(2)}) %collective-permute-start.9) | collective-permute-done | bytes 196640 | tf_op jit(solution)/shard_map/ppermute | solution.py:434
  64.4 2.8 %collective-permute-done.13.refs_15_ = bf16[384,256]{1,0:T(8,128)(2,1)S(1)} collective-permute-done((bf16[384,256]{1,0:T(8,128)(2,1)S(1)}, bf16[384,256]{1,0:T(8,128)(2,1)S(1)}, u32[]{:S(2)}, u32[]{:S(2)}) %collective-permute-start.13) | collective-permute-done | bytes 196640 | tf_op jit(solution)/shard_map/ppermute | solution.py:440
  67.2 3.2 %collective-permute-done.12.refs_14_ = bf16[384,256]{1,0:T(8,128)(2,1)S(1)} collective-permute-done((bf16[384,256]{1,0:T(8,128)(2,1)S(1)}, bf16[384,256]{1,0:T(8,128)(2,1)S(1)}, u32[]{:S(2)}, u32[]{:S(2)}) %collective-permute-start.12) | collective-permute-done | bytes 196640 | tf_op jit(solution)/shard_map/ppermute | solution.py:438
  71.7 8.6 %qkv.1 = (f32[768,256]{1,0:T(8,128)}, f32[768,256]{1,0:T(8,128)}, bf16[768,256]{1,0:T(8,128)(2,1)}, f32[2,768]{1,0:T(2,128)}) custom-call(s32[8]{0:T(128)} %get-tuple-element.29.order, bf16[384,256]{1,0:T(8,128)(2,1)} %copy-done.7, bf16[384,256]{1,0:T(8,128)(2,1)} %copy-done.6, bf16[384,256]{1,0:T(8,128)(2,1)} %copy-done.10, bf16[384,256]{1,0:T(8,128)(2,1)} %copy-done.11, ...), custom_call_target="tpu_custom_call" | custom-call | flops 2415919104 | bytes 9437184 | tf_op jit(solution)/shard_map/qkv/pallas_call | solution.py:142
  80.4 13.0 %psum.7.stat = f32[2,768]{1,0:T(2,128)} all-reduce(f32[2,768]{1,0:T(2,128)} %get-tuple-element.17), channel_id=1, replica_groups=mesh['req'=32,'tp'=8] {'tp'}, use_global_device_ids=true, to_apply=%region_1.2 | all-reduce | flops 1536 | bytes 12288 | tf_op jit(solution)/shard_map/psum | solution.py:518
  94.4 4.4 %collective-permute-start.15 = (bf16[256,2048]{1,0:T(8,128)(2,1)}, bf16[256,2048]{1,0:T(8,128)(2,1)}, u32[]{:S(2)}, u32[]{:S(2)}) collective-permute-start(bf16[256,2048]{1,0:T(8,128)(2,1)} %copy-done.4), channel_id=1, source_target_pairs={{0,8},{1,9},{2,10},{3,11},{4,12},{5,13},{6,14},{7,15},{8,0},{9,1},... | collective-permute-start | bytes 3145736 | tf_op jit(solution)/shard_map/ppermute | solution.py:509
  98.9 8.7 %collective-permute-done.18.refs_6_ = bf16[256,2048]{1,0:T(8,128)(2,1)S(1)} collective-permute-done((bf16[256,2048]{1,0:T(8,128)(2,1)}, bf16[256,2048]{1,0:T(8,128)(2,1)S(1)}, u32[]{:S(2)}, u32[]{:S(2)}) %collective-permute-start.18) | collective-permute-done | bytes 1048608 | tf_op jit(solution)/shard_map/ppermute | solution.py:509
  110.4 5.5 %collective-permute-start.19 = (bf16[256,2048]{1,0:T(8,128)(2,1)S(1)}, bf16[256,2048]{1,0:T(8,128)(2,1)}, u32[]{:S(2)}, u32[]{:S(2)}) collective-permute-start(bf16[256,2048]{1,0:T(8,128)(2,1)S(1)} %collective-permute-done.18.refs_6_), channel_id=1, source_target_pairs={{0,8},{1,9},{2,10},{3,11},{4,12},{5,13},{6,14},{7,15},{8,0},{9,1},... | collective-permute-start | bytes 3145736 | tf_op jit(solution)/shard_map/ppermute | solution.py:509
  117.1 16.5 %attend.1 = (bf16[768,256]{1,0:T(8,128)(2,1)}, bf16[768,256]{1,0:T(8,128)(2,1)}) custom-call(s32[1]{0:T(128)} %bitcast.1.place, s32[32]{0:T(128)} %lengths.3, s32[32,32]{1,0:T(8,128)} %page_table.1, f32[2,768]{1,0:T(2,128)} %psum.7.stat, bf16[1,256]{1,0:T(2,128)(2,1)} %broadcast_in_dim.31.q_gain, bf16[1,256]{1,0:T(2,128)(2,1)} %broadcast_in_dim.32.k_gain, ...), custom_call_target="tpu_custom_call" | custom-call | flops 3825205248 | bytes 9437184 | tf_op jit(solution)/shard_map/attend/pallas_call | solution.py:341
  133.6 4.5 %all-to-all-start.1 = ((bf16[8,96,256]{2,1,0:T(8,128)(2,1)}), bf16[8,96,256]{2,1,0:T(8,128)(2,1)S(1)}, u32[]{:S(2)}, u32[]{:S(2)}) async-start(bf16[8,96,256]{2,1,0:T(8,128)(2,1)} %bitcast.18), calls=%async_computation.1 | async-start | bytes 786432 | tf_op jit(solution)/shard_map/all_to_all | solution.py:542
  141.2 12.2 %all-to-all-done.1 = bf16[8,96,256]{2,1,0:T(8,128)(2,1)S(1)} async-done(((bf16[8,96,256]{2,1,0:T(8,128)(2,1)}), bf16[8,96,256]{2,1,0:T(8,128)(2,1)S(1)}, u32[]{:S(2)}, u32[]{:S(2)}) %all-to-all-start.1) | async-done | bytes 393248 | tf_op jit(solution)/shard_map/all_to_all | solution.py:542
  154.1 5.6 %project.1 = bf16[768,256]{1,0:T(8,128)(2,1)} custom-call(s32[9]{0:T(128)} %pad_add_fusion.order, bf16[768,256]{1,0:T(8,128)(2,1)} %bitcast.14, bf16[256,2048]{1,0:T(8,128)(2,1)} %refs_1_.1, bf16[256,2048]{1,0:T(8,128)(2,1)} %copy-done.4, bf16[256,2048]{1,0:T(8,128)(2,1)} %collective-permute-done.15.refs_3_, ...), custom_call_target="tpu_custom_call" | custom-call | flops 805306368 | bytes 9437184 | tf_op jit(solution)/shard_map/project/pallas_call | solution.py:408
  159.7 3.5 %all-to-all-start.2 = ((bf16[8,96,256]{2,1,0:T(8,128)(2,1)}), bf16[8,96,256]{2,1,0:T(8,128)(2,1)S(1)}, u32[]{:S(2)}, u32[]{:S(2)}) async-start(bf16[8,96,256]{2,1,0:T(8,128)(2,1)} %bitcast.15), calls=%async_computation.2 | async-start | bytes 786432 | tf_op jit(solution)/shard_map/all_to_all | solution.py:555
  163.2 15.0 %all-to-all-done.2 = bf16[8,96,256]{2,1,0:T(8,128)(2,1)S(1)} async-done(((bf16[8,96,256]{2,1,0:T(8,128)(2,1)}), bf16[8,96,256]{2,1,0:T(8,128)(2,1)S(1)}, u32[]{:S(2)}, u32[]{:S(2)}) %all-to-all-start.2) | async-done | bytes 393248 | tf_op jit(solution)/shard_map/all_to_all | solution.py:555
  (94 shorter events, 17.2 us)
Async XLA Ops:
  9.2 107.9 %all-to-all-start = ((bf16[32,256,256]{2,1,0:T(8,128)(2,1)}), bf16[32,256,256]{2,1,0:T(8,128)(2,1)}, u32[]{:S(2)}, u32[]{:S(2)}) async-start(bf16[32,256,256]{2,1,0:T(8,128)(2,1)} %get-tuple-element.15), calls=%async_computation | async-start | bytes 8388608 | tf_op jit(solution)/shard_map/all_to_all | solution.py:503
  17.8 52.5 %collective-permute-start.14 = (bf16[256,2048]{1,0:T(8,128)(2,1)S(1)}, bf16[256,2048]{1,0:T(8,128)(2,1)S(1)}, u32[]{:S(2)}, u32[]{:S(2)}) collective-permute-start(bf16[256,2048]{1,0:T(8,128)(2,1)S(1)} %copy-done.3), channel_id=1, source_target_pairs={{0,1},{1,2},{2,3},{3,4},{4,5},{5,6},{6,7},{7,0},{8,15},{9,8},{10,9... | collective-permute-start | bytes 3145736 | tf_op jit(solution)/shard_map/ppermute | solution.py:509
  23.5 20.1 %collective-permute-start.3 = (bf16[384,256]{1,0:T(8,128)(2,1)S(1)}, bf16[384,256]{1,0:T(8,128)(2,1)S(1)}, u32[]{:S(2)}, u32[]{:S(2)}) collective-permute-start(bf16[384,256]{1,0:T(8,128)(2,1)S(1)} %get-tuple-element.27.refs_1_), channel_id=1, source_target_pairs={{0,7},{1,0},{2,1},{3,2},{4,3},{5,4},{6,5},{7,6},{8,15},{9,8},{10,9... | collective-permute-start | bytes 589832 | tf_op jit(solution)/shard_map/ppermute | solution.py:435
  24.4 22.8 %collective-permute-start = (bf16[384,256]{1,0:T(8,128)(2,1)S(1)}, bf16[384,256]{1,0:T(8,128)(2,1)S(1)}, u32[]{:S(2)}, u32[]{:S(2)}) collective-permute-start(bf16[384,256]{1,0:T(8,128)(2,1)S(1)} %get-tuple-element.28.refs_0_), channel_id=1, source_target_pairs={{0,1},{1,2},{2,3},{3,4},{4,5},{5,6},{6,7},{7,0},{8,9},{9,10},{10,1... | collective-permute-start | bytes 589832 | tf_op jit(solution)/shard_map/ppermute | solution.py:434
  25.1 22.1 %collective-permute-start.1 = (bf16[384,256]{1,0:T(8,128)(2,1)S(1)}, bf16[384,256]{1,0:T(8,128)(2,1)S(1)}, u32[]{:S(2)}, u32[]{:S(2)}) collective-permute-start(bf16[384,256]{1,0:T(8,128)(2,1)S(1)} %get-tuple-element.27.refs_1_), channel_id=1, source_target_pairs={{0,1},{1,2},{2,3},{3,4},{4,5},{5,6},{6,7},{7,0},{8,9},{9,10},{10,1... | collective-permute-start | bytes 589832 | tf_op jit(solution)/shard_map/ppermute | solution.py:434
  25.1 22.2 %collective-permute-start.2 = (bf16[384,256]{1,0:T(8,128)(2,1)S(1)}, bf16[384,256]{1,0:T(8,128)(2,1)S(1)}, u32[]{:S(2)}, u32[]{:S(2)}) collective-permute-start(bf16[384,256]{1,0:T(8,128)(2,1)S(1)} %get-tuple-element.28.refs_0_), channel_id=1, source_target_pairs={{0,7},{1,0},{2,1},{3,2},{4,3},{5,4},{6,5},{7,6},{8,15},{9,8},{10,9... | collective-permute-start | bytes 589832 | tf_op jit(solution)/shard_map/ppermute | solution.py:435
  43.7 6.7 %collective-permute-start.7 = (bf16[384,256]{1,0:T(8,128)(2,1)S(1)}, bf16[384,256]{1,0:T(8,128)(2,1)S(1)}, u32[]{:S(2)}, u32[]{:S(2)}) collective-permute-start(bf16[384,256]{1,0:T(8,128)(2,1)S(1)} %collective-permute-done.3.refs_5_), channel_id=1, source_target_pairs={{0,7},{1,0},{2,1},{3,2},{4,3},{5,4},{6,5},{7,6},{8,15},{9,8},{10,9... | collective-permute-start | bytes 589832 | tf_op jit(solution)/shard_map/ppermute | solution.py:435
  47.2 6.8 %collective-permute-start.4 = (bf16[384,256]{1,0:T(8,128)(2,1)S(1)}, bf16[384,256]{1,0:T(8,128)(2,1)S(1)}, u32[]{:S(2)}, u32[]{:S(2)}) collective-permute-start(bf16[384,256]{1,0:T(8,128)(2,1)S(1)} %collective-permute-done.refs_2_), channel_id=1, source_target_pairs={{0,1},{1,2},{2,3},{3,4},{4,5},{5,6},{6,7},{7,0},{8,9},{9,10},{10,1... | collective-permute-start | bytes 589832 | tf_op jit(solution)/shard_map/ppermute | solution.py:434
  47.2 10.4 %collective-permute-start.5 = (bf16[384,256]{1,0:T(8,128)(2,1)S(1)}, bf16[384,256]{1,0:T(8,128)(2,1)S(1)}, u32[]{:S(2)}, u32[]{:S(2)}) collective-permute-start(bf16[384,256]{1,0:T(8,128)(2,1)S(1)} %collective-permute-done.1.refs_3_), channel_id=1, source_target_pairs={{0,1},{1,2},{2,3},{3,4},{4,5},{5,6},{6,7},{7,0},{8,9},{9,10},{10,1... | collective-permute-start | bytes 589832 | tf_op jit(solution)/shard_map/ppermute | solution.py:434
  47.3 10.3 %collective-permute-start.6 = (bf16[384,256]{1,0:T(8,128)(2,1)S(1)}, bf16[384,256]{1,0:T(8,128)(2,1)S(1)}, u32[]{:S(2)}, u32[]{:S(2)}) collective-permute-start(bf16[384,256]{1,0:T(8,128)(2,1)S(1)} %collective-permute-done.2.refs_4_), channel_id=1, source_target_pairs={{0,7},{1,0},{2,1},{3,2},{4,3},{5,4},{6,5},{7,6},{8,15},{9,8},{10,9... | collective-permute-start | bytes 589832 | tf_op jit(solution)/shard_map/ppermute | solution.py:435
  50.4 10.0 %collective-permute-start.11 = (bf16[384,256]{1,0:T(8,128)(2,1)S(1)}, bf16[384,256]{1,0:T(8,128)(2,1)S(1)}, u32[]{:S(2)}, u32[]{:S(2)}) collective-permute-start(bf16[384,256]{1,0:T(8,128)(2,1)S(1)} %collective-permute-done.7.refs_9_), channel_id=1, source_target_pairs={{0,7},{1,0},{2,1},{3,2},{4,3},{5,4},{6,5},{7,6},{8,15},{9,8},{10,9... | collective-permute-start | bytes 589832 | tf_op jit(solution)/shard_map/ppermute | solution.py:435
  54.0 8.2 %collective-permute-start.8 = (bf16[384,256]{1,0:T(8,128)(2,1)S(1)}, bf16[384,256]{1,0:T(8,128)(2,1)S(1)}, u32[]{:S(2)}, u32[]{:S(2)}) collective-permute-start(bf16[384,256]{1,0:T(8,128)(2,1)S(1)} %collective-permute-done.4.refs_6_), channel_id=1, source_target_pairs={{0,1},{1,2},{2,3},{3,4},{4,5},{5,6},{6,7},{7,0},{8,9},{9,10},{10,1... | collective-permute-start | bytes 589832 | tf_op jit(solution)/shard_map/ppermute | solution.py:434
  57.6 6.7 %collective-permute-start.9 = (bf16[384,256]{1,0:T(8,128)(2,1)S(1)}, bf16[384,256]{1,0:T(8,128)(2,1)S(1)}, u32[]{:S(2)}, u32[]{:S(2)}) collective-permute-start(bf16[384,256]{1,0:T(8,128)(2,1)S(1)} %collective-permute-done.5.refs_7_), channel_id=1, source_target_pairs={{0,1},{1,2},{2,3},{3,4},{4,5},{5,6},{6,7},{7,0},{8,9},{9,10},{10,1... | collective-permute-start | bytes 589832 | tf_op jit(solution)/shard_map/ppermute | solution.py:434
  57.7 6.7 %collective-permute-start.10 = (bf16[384,256]{1,0:T(8,128)(2,1)S(1)}, bf16[384,256]{1,0:T(8,128)(2,1)S(1)}, u32[]{:S(2)}, u32[]{:S(2)}) collective-permute-start(bf16[384,256]{1,0:T(8,128)(2,1)S(1)} %collective-permute-done.6.refs_8_), channel_id=1, source_target_pairs={{0,7},{1,0},{2,1},{3,2},{4,3},{5,4},{6,5},{7,6},{8,15},{9,8},{10,9... | collective-permute-start | bytes 589832 | tf_op jit(solution)/shard_map/ppermute | solution.py:435
  60.3 6.8 %collective-permute-start.13 = (bf16[384,256]{1,0:T(8,128)(2,1)S(1)}, bf16[384,256]{1,0:T(8,128)(2,1)S(1)}, u32[]{:S(2)}, u32[]{:S(2)}) collective-permute-start(bf16[384,256]{1,0:T(8,128)(2,1)S(1)} %collective-permute-done.11.refs_13_), channel_id=1, source_target_pairs={{0,7},{1,0},{2,1},{3,2},{4,3},{5,4},{6,5},{7,6},{8,15},{9,8},{10,9... | collective-permute-start | bytes 589832 | tf_op jit(solution)/shard_map/ppermute | solution.py:440
  62.2 8.1 %collective-permute-start.12 = (bf16[384,256]{1,0:T(8,128)(2,1)S(1)}, bf16[384,256]{1,0:T(8,128)(2,1)S(1)}, u32[]{:S(2)}, u32[]{:S(2)}) collective-permute-start(bf16[384,256]{1,0:T(8,128)(2,1)S(1)} %collective-permute-done.8.refs_10_), channel_id=1, source_target_pairs={{0,1},{1,2},{2,3},{3,4},{4,5},{5,6},{6,7},{7,0},{8,9},{9,10},{10,1... | collective-permute-start | bytes 589832 | tf_op jit(solution)/shard_map/ppermute | solution.py:438
  71.0 22.4 %collective-permute-start.16 = (bf16[256,2048]{1,0:T(8,128)(2,1)S(1)}, bf16[256,2048]{1,0:T(8,128)(2,1)}, u32[]{:S(2)}, u32[]{:S(2)}) collective-permute-start(bf16[256,2048]{1,0:T(8,128)(2,1)S(1)} %collective-permute-done.14.refs_2_), channel_id=1, source_target_pairs={{0,1},{1,2},{2,3},{3,4},{4,5},{5,6},{6,7},{7,0},{8,15},{9,8},{10,9... | collective-permute-start | bytes 3145736 | tf_op jit(solution)/shard_map/ppermute | solution.py:509
  93.4 14.2 %collective-permute-start.18 = (bf16[256,2048]{1,0:T(8,128)(2,1)}, bf16[256,2048]{1,0:T(8,128)(2,1)S(1)}, u32[]{:S(2)}, u32[]{:S(2)}) collective-permute-start(bf16[256,2048]{1,0:T(8,128)(2,1)} %collective-permute-done.16.refs_4_), channel_id=1, source_target_pairs={{0,1},{1,2},{2,3},{3,4},{4,5},{5,6},{6,7},{7,0},{8,15},{9,8},{10,9... | collective-permute-start | bytes 3145736 | tf_op jit(solution)/shard_map/ppermute | solution.py:509
  94.4 44.5 %collective-permute-start.15 = (bf16[256,2048]{1,0:T(8,128)(2,1)}, bf16[256,2048]{1,0:T(8,128)(2,1)}, u32[]{:S(2)}, u32[]{:S(2)}) collective-permute-start(bf16[256,2048]{1,0:T(8,128)(2,1)} %copy-done.4), channel_id=1, source_target_pairs={{0,8},{1,9},{2,10},{3,11},{4,12},{5,13},{6,14},{7,15},{8,0},{9,1},... | collective-permute-start | bytes 3145736 | tf_op jit(solution)/shard_map/ppermute | solution.py:509
  98.8 40.2 %collective-permute-start.17 = (bf16[256,2048]{1,0:T(8,128)(2,1)}, bf16[256,2048]{1,0:T(8,128)(2,1)}, u32[]{:S(2)}, u32[]{:S(2)}) collective-permute-start(bf16[256,2048]{1,0:T(8,128)(2,1)} %collective-permute-done.16.refs_4_), channel_id=1, source_target_pairs={{0,8},{1,9},{2,10},{3,11},{4,12},{5,13},{6,14},{7,15},{8,0},{9,1},... | collective-permute-start | bytes 3145736 | tf_op jit(solution)/shard_map/ppermute | solution.py:509
  108.4 29.7 %collective-permute-start.20 = (bf16[128,2048]{1,0:T(8,128)(2,1)}, bf16[128,2048]{1,0:T(8,128)(2,1)}, u32[]{:S(2)}, u32[]{:S(2)}) collective-permute-start(bf16[128,2048]{1,0:T(8,128)(2,1)} %constant_dynamic-slice_fusion), channel_id=1, source_target_pairs={{0,1},{1,2},{2,3},{3,4},{4,5},{5,6},{6,7},{7,0},{8,15},{9,8},{10,9... | collective-permute-start | bytes 1572872 | tf_op jit(solution)/shard_map/ppermute | solution.py:509
  110.4 30.8 %collective-permute-start.19 = (bf16[256,2048]{1,0:T(8,128)(2,1)S(1)}, bf16[256,2048]{1,0:T(8,128)(2,1)}, u32[]{:S(2)}, u32[]{:S(2)}) collective-permute-start(bf16[256,2048]{1,0:T(8,128)(2,1)S(1)} %collective-permute-done.18.refs_6_), channel_id=1, source_target_pairs={{0,8},{1,9},{2,10},{3,11},{4,12},{5,13},{6,14},{7,15},{8,0},{9,1},... | collective-permute-start | bytes 3145736 | tf_op jit(solution)/shard_map/ppermute | solution.py:509
  133.6 19.8 %all-to-all-start.1 = ((bf16[8,96,256]{2,1,0:T(8,128)(2,1)}), bf16[8,96,256]{2,1,0:T(8,128)(2,1)S(1)}, u32[]{:S(2)}, u32[]{:S(2)}) async-start(bf16[8,96,256]{2,1,0:T(8,128)(2,1)} %bitcast.18), calls=%async_computation.1 | async-start | bytes 786432 | tf_op jit(solution)/shard_map/all_to_all | solution.py:542
  159.7 18.5 %all-to-all-start.2 = ((bf16[8,96,256]{2,1,0:T(8,128)(2,1)}), bf16[8,96,256]{2,1,0:T(8,128)(2,1)S(1)}, u32[]{:S(2)}, u32[]{:S(2)}) async-start(bf16[8,96,256]{2,1,0:T(8,128)(2,1)} %bitcast.15), calls=%async_computation.2 | async-start | bytes 786432 | tf_op jit(solution)/shard_map/all_to_all | solution.py:555
  (27 other events, 513.3 us)
where the time goes:
time: 180 us; the launch traced here: 179 us
  waiting for transfers between devices  65.9 us (37%)
  starting transfers between devices  53.5 us (30%)
  Pallas kernels  37.3 us (21%)
  blocking collectives  13 us (7%)
  local copies, waits for them, and re-layouts  4.36 us (2%)
  other arithmetic  4.11 us (2%)
    ppermute x8, starting transfers between devices, move(): return lax.ppermute(value, axes, pairs)  18.7 us
    pallas_call x1, Pallas kernels, attend(): pl.pallas_call(functools.partial(attend_kernel, full), out_shape=(shape,...  16.5 us
    ppermute x6, waiting for transfers between devices, ring_gather(): backward[at] = lax.ppermute(backward[at], 'tp', left)  16.3 us
    ppermute x6, starting transfers between devices, ring_gather(): backward[at] = lax.ppermute(backward[at], 'tp', left)  15.8 us
    all_to_all x1, waiting for transfers between devices, body(): lax.all_to_all(normed, 'tp', split_axis=0, concat_axis=0, tiled=True)  15 us
    psum x1, blocking collectives, body(): stat = lax.psum(stat, 'tp')  13 us
    all_to_all x1, waiting for transfers between devices, body(): lax.all_to_all(attended, 'tp', split_axis=0, concat_axis=0, tiled=True)  12.2 us
    ppermute x8, waiting for transfers between devices, move(): return lax.ppermute(value, axes, pairs)  10.1 us
  transfers between devices with their start and end apart: 25, of which 12 were waited for; matrix products, arithmetic and copies ran while one was open for 2% of the time, Pallas kernels for 14%

commit v1 on v0

--- a/solution.py
+++ b/solution.py
@@ -91,7 +91,9 @@
 
 def qkv_kernel(count, parts, order, *refs):
     blocks = refs[: count * parts]
-    wq, wk, wv, q_out, k_out, v_out, stat, x, w, sem, w_sem = refs[count * parts :]
+    wq, wk, wv, q_out, k_out, v_out, stat, x, w, raw, values, sem, w_sem, out_sem = refs[
+        count * parts :
+    ]
     depth = x.shape[2]
     rows = x.shape[1]
     piece = rows // parts
@@ -99,38 +101,56 @@
     def weight_copy(which, source):
         return pltpu.make_async_copy(source, w.at[which], w_sem.at[which])
 
-    def block_copy(at, part):
+    def part_copy(at, part):
         return pltpu.make_async_copy(
-            blocks[at * parts + part], x.at[at, pl.ds(part * piece, piece)], sem.at[at, part]
+            blocks[at * parts + part], x.at[at, pl.ds(part * piece, piece)], sem.at[part]
         )
+
+    def part_wait(part):
+        whole = x.at[:, pl.ds(part * piece, piece)]
+        pltpu.make_async_copy(whole, whole, sem.at[part]).wait()
 
     weight_copy(0, wq).start()
     for at in range(count):
-        block_copy(at, 0).start()
+        part_copy(at, 0).start()
     weight_copy(1, wk).start()
     weight_copy(2, wv).start()
     for part in range(1, parts):
         for at in range(count):
-            block_copy(at, part).start()
+            part_copy(at, part).start()
     tile = 256
     ready = 0
+    leaving = []
     for start in range(0, rows, tile):
         here = slice(start, start + tile)
         needed = -(-(start + tile) // piece)
-        for which, (source, out) in enumerate(((wq, q_out), (wk, k_out), (wv, v_out))):
+        for which, source in enumerate((wq, wk, wv)):
             if start == 0:
                 weight_copy(which, source).wait()
+            for part in range(ready, needed):
+                part_wait(part)
+            ready = needed
             total = None
             for at in range(count):
-                for part in range(ready, needed):
-                    block_copy(at, part).wait()
                 span = pl.ds(pl.multiple_of(order[at] * depth, depth), depth)
                 term = jnp.dot(x[at, here, :], w[which, span, :], preferred_element_type=F32)
                 total = term if total is None else total + term
-            ready = needed
-            out[here, :] = total.astype(out.dtype)
             if which < 2:
+                raw[which, here, :] = total
                 stat[which : which + 1, here] = row_sums(total)
+                held, out = raw.at[which], (q_out, k_out)[which]
+            else:
+                values[here, :] = total.astype(BF16)
+                held, out = values, v_out
+            span = pl.ds(start, tile)
+            leaving.append(
+                pltpu.make_async_copy(
+                    held.at[span], out.at[span], out_sem.at[which, start // tile]
+                )
+            )
+            leaving[-1].start()
+    for copy in leaving:
+        copy.wait()
 
 
 def qkv(order, blocks, wq, wk, wv):
@@ -148,12 +168,15 @@
             jax.ShapeDtypeStruct((2, rows), F32),
         ),
         in_specs=[SMEM_SPEC] + [HBM_SPEC] * (count * parts + 3),
-        out_specs=(VMEM_SPEC,) * 4,
+        out_specs=(HBM_SPEC, HBM_SPEC, HBM_SPEC, VMEM_SPEC),
         scratch_shapes=[
             pltpu.VMEM((count, rows, depth), BF16),
             pltpu.VMEM((3, wq.shape[0], columns), BF16),
-            pltpu.SemaphoreType.DMA((count, parts)),
+            pltpu.VMEM((2, rows, columns), F32),
+            pltpu.VMEM((rows, columns), BF16),
+            pltpu.SemaphoreType.DMA((parts,)),
             pltpu.SemaphoreType.DMA((3,)),
+            pltpu.SemaphoreType.DMA((3, rows // 256)),
         ],
         compiler_params=params(62),
         cost_estimate=cost(2 * rows * depth * count * 3 * columns, 9 << 20),
@@ -189,9 +212,11 @@
     pages,
     ones,
     scores,
+    result_rows,
     counts,
     sem,
     page_sem,
+    out_sem,
 ):
     tile = 256
     slots = pages.shape[0]
@@ -249,7 +274,7 @@
             scale = lax.rsqrt(down_rows(stat[which : which + 1, here]) / full + EPSILON)
             for low in range(0, columns, HEAD_DIM):
                 lanes = slice(low, low + HEAD_DIM)
-                value = raw[which, here, lanes] * scale * gain[0:1, lanes].astype(F32)
+                value = raw[which, here, lanes] * scale * gain[lanes].astype(F32)[None]
                 turned = value * table[0, here, :]
                 turned = turned + pltpu.roll(value, HEAD_DIM // 2, 1) * table[1, here, :]
                 turned = turned.astype(BF16)
@@ -257,7 +282,8 @@
                     query[here, lanes] = turned
                 else:
                     new_k[here, lanes] = turned
-                    keys_out[here, lanes] = turned
+    leaving = [pltpu.make_async_copy(new_k, keys_out, out_sem.at[0])]
+    leaving[0].start()
     small[4].wait()
     for copy in parts:
         copy.wait()
@@ -327,7 +353,17 @@
                 v = jnp.concatenate([new_v[low : low + tile, head], one], 1)
                 result = result + jnp.dot(raised.astype(BF16), v, preferred_element_type=F32)
             result = result[:, :HEAD_DIM] / result[:, HEAD_DIM:]
-            out[start : start + tile, head] = result.astype(BF16)
+            result_rows[start : start + tile, head] = result.astype(BF16)
+            if column + HEAD_DIM == columns:
+                here = pl.ds(start, tile)
+                leaving.append(
+                    pltpu.make_async_copy(
+                        result_rows.at[here], out.at[here], out_sem.at[1 + start // tile]
+                    )
+                )
+                leaving[-1].start()
+    for copy in leaving:
+        copy.wait()
 
 
 def attend(
@@ -342,7 +378,7 @@
         functools.partial(attend_kernel, full),
         out_shape=(shape, shape),
         in_specs=[SMEM_SPEC] * 3 + [VMEM_SPEC] * 3 + [HBM_SPEC] * 6,
-        out_specs=(VMEM_SPEC, VMEM_SPEC),
+        out_specs=(HBM_SPEC, HBM_SPEC),
         scratch_shapes=[
             pltpu.VMEM((2, rows, columns), F32),
             pltpu.VMEM((2, rows, HEAD_DIM), F32),
@@ -352,9 +388,11 @@
             pltpu.VMEM((slots, both, columns), BF16),
             pltpu.VMEM((slots, both // 2, HEAD_DIM), BF16),
             pltpu.VMEM((256, keys), F32),
+            held,
             pltpu.SMEM((slots,), jnp.int32),
             pltpu.SemaphoreType.DMA((5,)),
             pltpu.SemaphoreType.DMA((slots,)),
+            pltpu.SemaphoreType.DMA((1 + rows // 256,)),
         ],
         compiler_params=params(62),
         cost_estimate=cost(4 * rows * keys * columns, 9 << 20),
@@ -525,8 +563,8 @@
         cache_len,
         page_table,
         stat,
-        q_gain[None],
-        k_gain[None],
+        q_gain,
+        k_gain,
         q_proj,
         k_proj,
         new_values,
@@ -549,9 +587,7 @@
     steps.append(size // 2)
     weight_order = (me + turn * jnp.array(steps, jnp.int32) + size) % size
     weight_order = jnp.concatenate([weight_order, core[None].astype(jnp.int32)])
-    normed = project(
-        weight_order, heads, [o_weight, o_1, s_1, o_2, s_2, o_3, s_3], o_4, s_4
-    )
+    normed = project(weight_order, heads, [o_weight, o_1, s_1, o_2, s_2, o_3, s_3], o_4, s_4)
     normed = lax.all_to_all(normed, "tp", split_axis=0, concat_axis=0, tiled=True)
     mixed = flat.astype(F32) + normed.astype(F32) * post_gain.astype(F32)
     return (mixed.astype(BF16)[None], new_keys[None], new_values[None])

time: 180 us -> 178 us (0.989)
  transfers between devices with their start and end apart: 25 -> 25, of which waited for: 12 -> 12; matrix products, arithmetic and copies ran while one was open for 2% -> 1% of each run, Pallas kernels for 14% -> 14%
where the time goes in v1:
time: 178 us; the launch traced here: 177 us
  waiting for transfers between devices  65.8 us (37%)
  starting transfers between devices  53.7 us (30%)
  Pallas kernels  36.4 us (20%)
  blocking collectives  13 us (7%)
  other arithmetic  4.02 us (2%)
  local copies, waits for them, and re-layouts  3.2 us (2%)
    ppermute x8, starting transfers between devices, move(): return lax.ppermute(value, axes, pairs)  18.8 us
    pallas_call x1, Pallas kernels, attend(): pl.pallas_call(functools.partial(attend_kernel, full), out_shape=(shape,...  16.4 us
    ppermute x6, waiting for transfers between devices, ring_gather(): backward[at] = lax.ppermute(backward[at], 'tp', left)  16.3 us
    ppermute x6, starting transfers between devices, ring_gather(): backward[at] = lax.ppermute(backward[at], 'tp', left)  15.8 us
    all_to_all x1, waiting for transfers between devices, body(): lax.all_to_all(normed, 'tp', split_axis=0, concat_axis=0, tiled=True)  15 us
    psum x1, blocking collectives, body(): stat = lax.psum(stat, 'tp')  13 us
    all_to_all x1, waiting for transfers between devices, body(): lax.all_to_all(attended, 'tp', split_axis=0, concat_axis=0, tiled=True)  12.2 us
    ppermute x8, waiting for transfers between devices, move(): return lax.ppermute(value, axes, pairs)  10.1 us
  transfers between devices with their start and end apart: 25, of which 12 were waited for; matrix products, arithmetic and copies ran while one was open for 1% of the time, Pallas kernels for 14%

profile of v1, /device:TPU:1, one launch (start us, length us, event | category | flops | bytes accessed | tf_op | source)
XLA Modules:
  0.0 177.1 jit_solution(10431866319538727925)
XLA Ops:
  2.6 6.5 %pick_pages.1 = (bf16[32,256,256]{2,1,0:T(8,128)(2,1)}, f32[768,128]{1,0:T(8,128)}, f32[768,128]{1,0:T(8,128)}) custom-call(s32[32]{0:T(128)} %fusion.6.chosen, s32[1]{0:T(128)} %bitcast.1.place, s32[32]{0:T(128)} %lengths.3, f32[1,128]{1,0:T(1,128)} %maximum_bitcast_fusion.freqs, bf16[32,128,256]{2,1,0:T(8,128)(2,1)} %key_pool.1, ...), custom_call_target="tpu_custom_call" | custom-call | tf_op jit(solution)/shard_map/pick_pages/pallas_call | solution.py:66
  9.2 8.6 %all-to-all-start = ((bf16[32,256,256]{2,1,0:T(8,128)(2,1)}), bf16[32,256,256]{2,1,0:T(8,128)(2,1)}, u32[]{:S(2)}, u32[]{:S(2)}) async-start(bf16[32,256,256]{2,1,0:T(8,128)(2,1)} %get-tuple-element.15), calls=%async_computation | async-start | bytes 8388608 | tf_op jit(solution)/shard_map/all_to_all | solution.py:541
  17.8 5.7 %collective-permute-start.14 = (bf16[256,2048]{1,0:T(8,128)(2,1)S(1)}, bf16[256,2048]{1,0:T(8,128)(2,1)S(1)}, u32[]{:S(2)}, u32[]{:S(2)}) collective-permute-start(bf16[256,2048]{1,0:T(8,128)(2,1)S(1)} %copy-done.3), channel_id=1, source_target_pairs={{0,1},{1,2},{2,3},{3,4},{4,5},{5,6},{6,7},{7,0},{8,15},{9,8},{10,9... | collective-permute-start | bytes 3145736 | tf_op jit(solution)/shard_map/ppermute | solution.py:547
  25.1 2.7 %collective-permute-start.2 = (bf16[384,256]{1,0:T(8,128)(2,1)S(1)}, bf16[384,256]{1,0:T(8,128)(2,1)S(1)}, u32[]{:S(2)}, u32[]{:S(2)}) collective-permute-start(bf16[384,256]{1,0:T(8,128)(2,1)S(1)} %get-tuple-element.28.refs_0_), channel_id=1, source_target_pairs={{0,7},{1,0},{2,1},{3,2},{4,3},{5,4},{6,5},{7,6},{8,15},{9,8},{10,9... | collective-permute-start | bytes 589832 | tf_op jit(solution)/shard_map/ppermute | solution.py:473
  27.8 15.9 %collective-permute-done.3.refs_5_ = bf16[384,256]{1,0:T(8,128)(2,1)S(1)} collective-permute-done((bf16[384,256]{1,0:T(8,128)(2,1)S(1)}, bf16[384,256]{1,0:T(8,128)(2,1)S(1)}, u32[]{:S(2)}, u32[]{:S(2)}) %collective-permute-start.3) | collective-permute-done | bytes 196640 | tf_op jit(solution)/shard_map/ppermute | solution.py:473
  43.7 3.5 %collective-permute-start.7 = (bf16[384,256]{1,0:T(8,128)(2,1)S(1)}, bf16[384,256]{1,0:T(8,128)(2,1)S(1)}, u32[]{:S(2)}, u32[]{:S(2)}) collective-permute-start(bf16[384,256]{1,0:T(8,128)(2,1)S(1)} %collective-permute-done.3.refs_5_), channel_id=1, source_target_pairs={{0,7},{1,0},{2,1},{3,2},{4,3},{5,4},{6,5},{7,6},{8,15},{9,8},{10,9... | collective-permute-start | bytes 589832 | tf_op jit(solution)/shard_map/ppermute | solution.py:473
  47.3 2.6 %collective-permute-start.6 = (bf16[384,256]{1,0:T(8,128)(2,1)S(1)}, bf16[384,256]{1,0:T(8,128)(2,1)S(1)}, u32[]{:S(2)}, u32[]{:S(2)}) collective-permute-start(bf16[384,256]{1,0:T(8,128)(2,1)S(1)} %collective-permute-done.2.refs_4_), channel_id=1, source_target_pairs={{0,7},{1,0},{2,1},{3,2},{4,3},{5,4},{6,5},{7,6},{8,15},{9,8},{10,9... | collective-permute-start | bytes 589832 | tf_op jit(solution)/shard_map/ppermute | solution.py:473
  50.4 3.5 %collective-permute-start.11 = (bf16[384,256]{1,0:T(8,128)(2,1)S(1)}, bf16[384,256]{1,0:T(8,128)(2,1)S(1)}, u32[]{:S(2)}, u32[]{:S(2)}) collective-permute-start(bf16[384,256]{1,0:T(8,128)(2,1)S(1)} %collective-permute-done.7.refs_9_), channel_id=1, source_target_pairs={{0,7},{1,0},{2,1},{3,2},{4,3},{5,4},{6,5},{7,6},{8,15},{9,8},{10,9... | collective-permute-start | bytes 589832 | tf_op jit(solution)/shard_map/ppermute | solution.py:473
  54.0 3.6 %collective-permute-done.5.refs_7_ = bf16[384,256]{1,0:T(8,128)(2,1)S(1)} collective-permute-done((bf16[384,256]{1,0:T(8,128)(2,1)S(1)}, bf16[384,256]{1,0:T(8,128)(2,1)S(1)}, u32[]{:S(2)}, u32[]{:S(2)}) %collective-permute-start.5) | collective-permute-done | bytes 196640 | tf_op jit(solution)/shard_map/ppermute | solution.py:472
  57.6 2.7 %collective-permute-start.10 = (bf16[384,256]{1,0:T(8,128)(2,1)S(1)}, bf16[384,256]{1,0:T(8,128)(2,1)S(1)}, u32[]{:S(2)}, u32[]{:S(2)}) collective-permute-start(bf16[384,256]{1,0:T(8,128)(2,1)S(1)} %collective-permute-done.6.refs_8_), channel_id=1, source_target_pairs={{0,7},{1,0},{2,1},{3,2},{4,3},{5,4},{6,5},{7,6},{8,15},{9,8},{10,9... | collective-permute-start | bytes 589832 | tf_op jit(solution)/shard_map/ppermute | solution.py:473
  64.4 2.8 %collective-permute-done.13.refs_15_ = bf16[384,256]{1,0:T(8,128)(2,1)S(1)} collective-permute-done((bf16[384,256]{1,0:T(8,128)(2,1)S(1)}, bf16[384,256]{1,0:T(8,128)(2,1)S(1)}, u32[]{:S(2)}, u32[]{:S(2)}) %collective-permute-start.13) | collective-permute-done | bytes 196640 | tf_op jit(solution)/shard_map/ppermute | solution.py:478
  67.1 3.2 %collective-permute-done.12.refs_14_ = bf16[384,256]{1,0:T(8,128)(2,1)S(1)} collective-permute-done((bf16[384,256]{1,0:T(8,128)(2,1)S(1)}, bf16[384,256]{1,0:T(8,128)(2,1)S(1)}, u32[]{:S(2)}, u32[]{:S(2)}) %collective-permute-start.12) | collective-permute-done | bytes 196640 | tf_op jit(solution)/shard_map/ppermute | solution.py:476
  71.6 7.9 %qkv.1 = (f32[768,256]{1,0:T(8,128)}, f32[768,256]{1,0:T(8,128)}, bf16[768,256]{1,0:T(8,128)(2,1)}, f32[2,768]{1,0:T(2,128)}) custom-call(s32[8]{0:T(128)} %get-tuple-element.29.order, bf16[384,256]{1,0:T(8,128)(2,1)} %copy-done.7, bf16[384,256]{1,0:T(8,128)(2,1)} %copy-done.6, bf16[384,256]{1,0:T(8,128)(2,1)} %copy-done.10, bf16[384,256]{1,0:T(8,128)(2,1)} %copy-done.11, ...), custom_call_target="tpu_custom_call" | custom-call | flops 2415919104 | bytes 9437184 | tf_op jit(solution)/shard_map/qkv/pallas_call | solution.py:162
  79.5 13.0 %psum.7.stat = f32[2,768]{1,0:T(2,128)} all-reduce(f32[2,768]{1,0:T(2,128)} %get-tuple-element.17), channel_id=1, replica_groups=mesh['req'=32,'tp'=8] {'tp'}, use_global_device_ids=true, to_apply=%region_1.2 | all-reduce | flops 1536 | bytes 12288 | tf_op jit(solution)/shard_map/psum | solution.py:556
  94.0 4.2 %collective-permute-start.15 = (bf16[256,2048]{1,0:T(8,128)(2,1)}, bf16[256,2048]{1,0:T(8,128)(2,1)}, u32[]{:S(2)}, u32[]{:S(2)}) collective-permute-start(bf16[256,2048]{1,0:T(8,128)(2,1)} %copy-done.4), channel_id=1, source_target_pairs={{0,8},{1,9},{2,10},{3,11},{4,12},{5,13},{6,14},{7,15},{8,0},{9,1},... | collective-permute-start | bytes 3145736 | tf_op jit(solution)/shard_map/ppermute | solution.py:547
  98.2 8.5 %collective-permute-done.18.refs_6_ = bf16[256,2048]{1,0:T(8,128)(2,1)S(1)} collective-permute-done((bf16[256,2048]{1,0:T(8,128)(2,1)}, bf16[256,2048]{1,0:T(8,128)(2,1)S(1)}, u32[]{:S(2)}, u32[]{:S(2)}) %collective-permute-start.18) | collective-permute-done | bytes 1048608 | tf_op jit(solution)/shard_map/ppermute | solution.py:547
  107.6 2.4 %collective-permute-start.20 = (bf16[128,2048]{1,0:T(8,128)(2,1)}, bf16[128,2048]{1,0:T(8,128)(2,1)}, u32[]{:S(2)}, u32[]{:S(2)}) collective-permute-start(bf16[128,2048]{1,0:T(8,128)(2,1)} %constant_dynamic-slice_fusion), channel_id=1, source_target_pairs={{0,1},{1,2},{2,3},{3,4},{4,5},{5,6},{6,7},{7,0},{8,15},{9,8},{10,9... | collective-permute-start | bytes 1572872 | tf_op jit(solution)/shard_map/ppermute | solution.py:547
  110.0 5.1 %collective-permute-start.19 = (bf16[256,2048]{1,0:T(8,128)(2,1)S(1)}, bf16[256,2048]{1,0:T(8,128)(2,1)}, u32[]{:S(2)}, u32[]{:S(2)}) collective-permute-start(bf16[256,2048]{1,0:T(8,128)(2,1)S(1)} %collective-permute-done.18.refs_6_), channel_id=1, source_target_pairs={{0,8},{1,9},{2,10},{3,11},{4,12},{5,13},{6,14},{7,15},{8,0},{9,1},... | collective-permute-start | bytes 3145736 | tf_op jit(solution)/shard_map/ppermute | solution.py:547
  115.1 16.4 %attend.1 = (bf16[768,256]{1,0:T(8,128)(2,1)}, bf16[768,256]{1,0:T(8,128)(2,1)}) custom-call(s32[1]{0:T(128)} %bitcast.1.place, s32[32]{0:T(128)} %lengths.3, s32[32,32]{1,0:T(8,128)} %page_table.1, f32[2,768]{1,0:T(2,128)} %psum.7.stat, bf16[256]{0:T(256)(128)(2,1)} %q_gain.1, bf16[256]{0:T(256)(128)(2,1)} %k_gain.1, f32[768,256]{1,0:T(8,128)} %get-tuple-element.18.q_hbm, ...), custom_call_target="tpu_custom_call" | custom-call | flops 3825205248 | bytes 9437184 | tf_op jit(solution)/shard_map/attend/pallas_call | solution.py:377
  131.6 4.5 %all-to-all-start.1 = ((bf16[8,96,256]{2,1,0:T(8,128)(2,1)}), bf16[8,96,256]{2,1,0:T(8,128)(2,1)S(1)}, u32[]{:S(2)}, u32[]{:S(2)}) async-start(bf16[8,96,256]{2,1,0:T(8,128)(2,1)} %bitcast.18), calls=%async_computation.1 | async-start | bytes 786432 | tf_op jit(solution)/shard_map/all_to_all | solution.py:580
  139.1 12.2 %all-to-all-done.1 = bf16[8,96,256]{2,1,0:T(8,128)(2,1)S(1)} async-done(((bf16[8,96,256]{2,1,0:T(8,128)(2,1)}), bf16[8,96,256]{2,1,0:T(8,128)(2,1)S(1)}, u32[]{:S(2)}, u32[]{:S(2)}) %all-to-all-start.1) | async-done | bytes 393248 | tf_op jit(solution)/shard_map/all_to_all | solution.py:580
  152.1 5.6 %project.1 = bf16[768,256]{1,0:T(8,128)(2,1)} custom-call(s32[9]{0:T(128)} %pad_add_fusion.order, bf16[768,256]{1,0:T(8,128)(2,1)} %bitcast.14, bf16[256,2048]{1,0:T(8,128)(2,1)} %refs_1_.1, bf16[256,2048]{1,0:T(8,128)(2,1)} %copy-done.4, bf16[256,2048]{1,0:T(8,128)(2,1)} %collective-permute-done.15.refs_3_, ...), custom_call_target="tpu_custom_call" | custom-call | flops 805306368 | bytes 9437184 | tf_op jit(solution)/shard_map/project/pallas_call | solution.py:446
  157.6 3.5 %all-to-all-start.2 = ((bf16[8,96,256]{2,1,0:T(8,128)(2,1)}), bf16[8,96,256]{2,1,0:T(8,128)(2,1)S(1)}, u32[]{:S(2)}, u32[]{:S(2)}) async-start(bf16[8,96,256]{2,1,0:T(8,128)(2,1)} %bitcast.15), calls=%async_computation.2 | async-start | bytes 786432 | tf_op jit(solution)/shard_map/all_to_all | solution.py:591
  161.1 15.0 %all-to-all-done.2 = bf16[8,96,256]{2,1,0:T(8,128)(2,1)S(1)} async-done(((bf16[8,96,256]{2,1,0:T(8,128)(2,1)}), bf16[8,96,256]{2,1,0:T(8,128)(2,1)S(1)}, u32[]{:S(2)}, u32[]{:S(2)}) %all-to-all-start.2) | async-done | bytes 393248 | tf_op jit(solution)/shard_map/all_to_all | solution.py:591
  (88 shorter events, 16.5 us)
Async XLA Ops:
  9.2 105.9 %all-to-all-start = ((bf16[32,256,256]{2,1,0:T(8,128)(2,1)}), bf16[32,256,256]{2,1,0:T(8,128)(2,1)}, u32[]{:S(2)}, u32[]{:S(2)}) async-start(bf16[32,256,256]{2,1,0:T(8,128)(2,1)} %get-tuple-element.15), calls=%async_computation | async-start | bytes 8388608 | tf_op jit(solution)/shard_map/all_to_all | solution.py:541
  17.8 52.5 %collective-permute-start.14 = (bf16[256,2048]{1,0:T(8,128)(2,1)S(1)}, bf16[256,2048]{1,0:T(8,128)(2,1)S(1)}, u32[]{:S(2)}, u32[]{:S(2)}) collective-permute-start(bf16[256,2048]{1,0:T(8,128)(2,1)S(1)} %copy-done.3), channel_id=1, source_target_pairs={{0,1},{1,2},{2,3},{3,4},{4,5},{5,6},{6,7},{7,0},{8,15},{9,8},{10,9... | collective-permute-start | bytes 3145736 | tf_op jit(solution)/shard_map/ppermute | solution.py:547
  23.5 20.1 %collective-permute-start.3 = (bf16[384,256]{1,0:T(8,128)(2,1)S(1)}, bf16[384,256]{1,0:T(8,128)(2,1)S(1)}, u32[]{:S(2)}, u32[]{:S(2)}) collective-permute-start(bf16[384,256]{1,0:T(8,128)(2,1)S(1)} %get-tuple-element.27.refs_1_), channel_id=1, source_target_pairs={{0,7},{1,0},{2,1},{3,2},{4,3},{5,4},{6,5},{7,6},{8,15},{9,8},{10,9... | collective-permute-start | bytes 589832 | tf_op jit(solution)/shard_map/ppermute | solution.py:473
  24.3 22.8 %collective-permute-start = (bf16[384,256]{1,0:T(8,128)(2,1)S(1)}, bf16[384,256]{1,0:T(8,128)(2,1)S(1)}, u32[]{:S(2)}, u32[]{:S(2)}) collective-permute-start(bf16[384,256]{1,0:T(8,128)(2,1)S(1)} %get-tuple-element.28.refs_0_), channel_id=1, source_target_pairs={{0,1},{1,2},{2,3},{3,4},{4,5},{5,6},{6,7},{7,0},{8,9},{9,10},{10,1... | collective-permute-start | bytes 589832 | tf_op jit(solution)/shard_map/ppermute | solution.py:472
  25.1 22.1 %collective-permute-start.1 = (bf16[384,256]{1,0:T(8,128)(2,1)S(1)}, bf16[384,256]{1,0:T(8,128)(2,1)S(1)}, u32[]{:S(2)}, u32[]{:S(2)}) collective-permute-start(bf16[384,256]{1,0:T(8,128)(2,1)S(1)} %get-tuple-element.27.refs_1_), channel_id=1, source_target_pairs={{0,1},{1,2},{2,3},{3,4},{4,5},{5,6},{6,7},{7,0},{8,9},{9,10},{10,1... | collective-permute-start | bytes 589832 | tf_op jit(solution)/shard_map/ppermute | solution.py:472
  25.1 22.2 %collective-permute-start.2 = (bf16[384,256]{1,0:T(8,128)(2,1)S(1)}, bf16[384,256]{1,0:T(8,128)(2,1)S(1)}, u32[]{:S(2)}, u32[]{:S(2)}) collective-permute-start(bf16[384,256]{1,0:T(8,128)(2,1)S(1)} %get-tuple-element.28.refs_0_), channel_id=1, source_target_pairs={{0,7},{1,0},{2,1},{3,2},{4,3},{5,4},{6,5},{7,6},{8,15},{9,8},{10,9... | collective-permute-start | bytes 589832 | tf_op jit(solution)/shard_map/ppermute | solution.py:473
  43.7 6.7 %collective-permute-start.7 = (bf16[384,256]{1,0:T(8,128)(2,1)S(1)}, bf16[384,256]{1,0:T(8,128)(2,1)S(1)}, u32[]{:S(2)}, u32[]{:S(2)}) collective-permute-start(bf16[384,256]{1,0:T(8,128)(2,1)S(1)} %collective-permute-done.3.refs_5_), channel_id=1, source_target_pairs={{0,7},{1,0},{2,1},{3,2},{4,3},{5,4},{6,5},{7,6},{8,15},{9,8},{10,9... | collective-permute-start | bytes 589832 | tf_op jit(solution)/shard_map/ppermute | solution.py:473
  47.2 6.8 %collective-permute-start.4 = (bf16[384,256]{1,0:T(8,128)(2,1)S(1)}, bf16[384,256]{1,0:T(8,128)(2,1)S(1)}, u32[]{:S(2)}, u32[]{:S(2)}) collective-permute-start(bf16[384,256]{1,0:T(8,128)(2,1)S(1)} %collective-permute-done.refs_2_), channel_id=1, source_target_pairs={{0,1},{1,2},{2,3},{3,4},{4,5},{5,6},{6,7},{7,0},{8,9},{9,10},{10,1... | collective-permute-start | bytes 589832 | tf_op jit(solution)/shard_map/ppermute | solution.py:472
  47.2 10.4 %collective-permute-start.5 = (bf16[384,256]{1,0:T(8,128)(2,1)S(1)}, bf16[384,256]{1,0:T(8,128)(2,1)S(1)}, u32[]{:S(2)}, u32[]{:S(2)}) collective-permute-start(bf16[384,256]{1,0:T(8,128)(2,1)S(1)} %collective-permute-done.1.refs_3_), channel_id=1, source_target_pairs={{0,1},{1,2},{2,3},{3,4},{4,5},{5,6},{6,7},{7,0},{8,9},{9,10},{10,1... | collective-permute-start | bytes 589832 | tf_op jit(solution)/shard_map/ppermute | solution.py:472
  47.3 10.3 %collective-permute-start.6 = (bf16[384,256]{1,0:T(8,128)(2,1)S(1)}, bf16[384,256]{1,0:T(8,128)(2,1)S(1)}, u32[]{:S(2)}, u32[]{:S(2)}) collective-permute-start(bf16[384,256]{1,0:T(8,128)(2,1)S(1)} %collective-permute-done.2.refs_4_), channel_id=1, source_target_pairs={{0,7},{1,0},{2,1},{3,2},{4,3},{5,4},{6,5},{7,6},{8,15},{9,8},{10,9... | collective-permute-start | bytes 589832 | tf_op jit(solution)/shard_map/ppermute | solution.py:473
  50.4 10.0 %collective-permute-start.11 = (bf16[384,256]{1,0:T(8,128)(2,1)S(1)}, bf16[384,256]{1,0:T(8,128)(2,1)S(1)}, u32[]{:S(2)}, u32[]{:S(2)}) collective-permute-start(bf16[384,256]{1,0:T(8,128)(2,1)S(1)} %collective-permute-done.7.refs_9_), channel_id=1, source_target_pairs={{0,7},{1,0},{2,1},{3,2},{4,3},{5,4},{6,5},{7,6},{8,15},{9,8},{10,9... | collective-permute-start | bytes 589832 | tf_op jit(solution)/shard_map/ppermute | solution.py:473
  54.0 8.2 %collective-permute-start.8 = (bf16[384,256]{1,0:T(8,128)(2,1)S(1)}, bf16[384,256]{1,0:T(8,128)(2,1)S(1)}, u32[]{:S(2)}, u32[]{:S(2)}) collective-permute-start(bf16[384,256]{1,0:T(8,128)(2,1)S(1)} %collective-permute-done.4.refs_6_), channel_id=1, source_target_pairs={{0,1},{1,2},{2,3},{3,4},{4,5},{5,6},{6,7},{7,0},{8,9},{9,10},{10,1... | collective-permute-start | bytes 589832 | tf_op jit(solution)/shard_map/ppermute | solution.py:472
  57.6 6.7 %collective-permute-start.9 = (bf16[384,256]{1,0:T(8,128)(2,1)S(1)}, bf16[384,256]{1,0:T(8,128)(2,1)S(1)}, u32[]{:S(2)}, u32[]{:S(2)}) collective-permute-start(bf16[384,256]{1,0:T(8,128)(2,1)S(1)} %collective-permute-done.5.refs_7_), channel_id=1, source_target_pairs={{0,1},{1,2},{2,3},{3,4},{4,5},{5,6},{6,7},{7,0},{8,9},{9,10},{10,1... | collective-permute-start | bytes 589832 | tf_op jit(solution)/shard_map/ppermute | solution.py:472
  57.6 6.7 %collective-permute-start.10 = (bf16[384,256]{1,0:T(8,128)(2,1)S(1)}, bf16[384,256]{1,0:T(8,128)(2,1)S(1)}, u32[]{:S(2)}, u32[]{:S(2)}) collective-permute-start(bf16[384,256]{1,0:T(8,128)(2,1)S(1)} %collective-permute-done.6.refs_8_), channel_id=1, source_target_pairs={{0,7},{1,0},{2,1},{3,2},{4,3},{5,4},{6,5},{7,6},{8,15},{9,8},{10,9... | collective-permute-start | bytes 589832 | tf_op jit(solution)/shard_map/ppermute | solution.py:473
  60.3 6.8 %collective-permute-start.13 = (bf16[384,256]{1,0:T(8,128)(2,1)S(1)}, bf16[384,256]{1,0:T(8,128)(2,1)S(1)}, u32[]{:S(2)}, u32[]{:S(2)}) collective-permute-start(bf16[384,256]{1,0:T(8,128)(2,1)S(1)} %collective-permute-done.11.refs_13_), channel_id=1, source_target_pairs={{0,7},{1,0},{2,1},{3,2},{4,3},{5,4},{6,5},{7,6},{8,15},{9,8},{10,9... | collective-permute-start | bytes 589832 | tf_op jit(solution)/shard_map/ppermute | solution.py:478
  62.2 8.1 %collective-permute-start.12 = (bf16[384,256]{1,0:T(8,128)(2,1)S(1)}, bf16[384,256]{1,0:T(8,128)(2,1)S(1)}, u32[]{:S(2)}, u32[]{:S(2)}) collective-permute-start(bf16[384,256]{1,0:T(8,128)(2,1)S(1)} %collective-permute-done.8.refs_10_), channel_id=1, source_target_pairs={{0,1},{1,2},{2,3},{3,4},{4,5},{5,6},{6,7},{7,0},{8,9},{9,10},{10,1... | collective-permute-start | bytes 589832 | tf_op jit(solution)/shard_map/ppermute | solution.py:476
  71.0 21.5 %collective-permute-start.16 = (bf16[256,2048]{1,0:T(8,128)(2,1)S(1)}, bf16[256,2048]{1,0:T(8,128)(2,1)}, u32[]{:S(2)}, u32[]{:S(2)}) collective-permute-start(bf16[256,2048]{1,0:T(8,128)(2,1)S(1)} %collective-permute-done.14.refs_2_), channel_id=1, source_target_pairs={{0,1},{1,2},{2,3},{3,4},{4,5},{5,6},{6,7},{7,0},{8,15},{9,8},{10,9... | collective-permute-start | bytes 3145736 | tf_op jit(solution)/shard_map/ppermute | solution.py:547
  92.5 14.2 %collective-permute-start.18 = (bf16[256,2048]{1,0:T(8,128)(2,1)}, bf16[256,2048]{1,0:T(8,128)(2,1)S(1)}, u32[]{:S(2)}, u32[]{:S(2)}) collective-permute-start(bf16[256,2048]{1,0:T(8,128)(2,1)} %collective-permute-done.16.refs_4_), channel_id=1, source_target_pairs={{0,1},{1,2},{2,3},{3,4},{4,5},{5,6},{6,7},{7,0},{8,15},{9,8},{10,9... | collective-permute-start | bytes 3145736 | tf_op jit(solution)/shard_map/ppermute | solution.py:547
  94.0 42.8 %collective-permute-start.15 = (bf16[256,2048]{1,0:T(8,128)(2,1)}, bf16[256,2048]{1,0:T(8,128)(2,1)}, u32[]{:S(2)}, u32[]{:S(2)}) collective-permute-start(bf16[256,2048]{1,0:T(8,128)(2,1)} %copy-done.4), channel_id=1, source_target_pairs={{0,8},{1,9},{2,10},{3,11},{4,12},{5,13},{6,14},{7,15},{8,0},{9,1},... | collective-permute-start | bytes 3145736 | tf_op jit(solution)/shard_map/ppermute | solution.py:547
  98.2 38.7 %collective-permute-start.17 = (bf16[256,2048]{1,0:T(8,128)(2,1)}, bf16[256,2048]{1,0:T(8,128)(2,1)}, u32[]{:S(2)}, u32[]{:S(2)}) collective-permute-start(bf16[256,2048]{1,0:T(8,128)(2,1)} %collective-permute-done.16.refs_4_), channel_id=1, source_target_pairs={{0,8},{1,9},{2,10},{3,11},{4,12},{5,13},{6,14},{7,15},{8,0},{9,1},... | collective-permute-start | bytes 3145736 | tf_op jit(solution)/shard_map/ppermute | solution.py:547
  107.6 28.5 %collective-permute-start.20 = (bf16[128,2048]{1,0:T(8,128)(2,1)}, bf16[128,2048]{1,0:T(8,128)(2,1)}, u32[]{:S(2)}, u32[]{:S(2)}) collective-permute-start(bf16[128,2048]{1,0:T(8,128)(2,1)} %constant_dynamic-slice_fusion), channel_id=1, source_target_pairs={{0,1},{1,2},{2,3},{3,4},{4,5},{5,6},{6,7},{7,0},{8,15},{9,8},{10,9... | collective-permute-start | bytes 1572872 | tf_op jit(solution)/shard_map/ppermute | solution.py:547
  110.0 29.1 %collective-permute-start.19 = (bf16[256,2048]{1,0:T(8,128)(2,1)S(1)}, bf16[256,2048]{1,0:T(8,128)(2,1)}, u32[]{:S(2)}, u32[]{:S(2)}) collective-permute-start(bf16[256,2048]{1,0:T(8,128)(2,1)S(1)} %collective-permute-done.18.refs_6_), channel_id=1, source_target_pairs={{0,8},{1,9},{2,10},{3,11},{4,12},{5,13},{6,14},{7,15},{8,0},{9,1},... | collective-permute-start | bytes 3145736 | tf_op jit(solution)/shard_map/ppermute | solution.py:547
  131.6 19.8 %all-to-all-start.1 = ((bf16[8,96,256]{2,1,0:T(8,128)(2,1)}), bf16[8,96,256]{2,1,0:T(8,128)(2,1)S(1)}, u32[]{:S(2)}, u32[]{:S(2)}) async-start(bf16[8,96,256]{2,1,0:T(8,128)(2,1)} %bitcast.18), calls=%async_computation.1 | async-start | bytes 786432 | tf_op jit(solution)/shard_map/all_to_all | solution.py:580
  157.6 18.5 %all-to-all-start.2 = ((bf16[8,96,256]{2,1,0:T(8,128)(2,1)}), bf16[8,96,256]{2,1,0:T(8,128)(2,1)S(1)}, u32[]{:S(2)}, u32[]{:S(2)}) async-start(bf16[8,96,256]{2,1,0:T(8,128)(2,1)} %bitcast.15), calls=%async_computation.2 | async-start | bytes 786432 | tf_op jit(solution)/shard_map/all_to_all | solution.py:591
  (25 other events, 422.0 us)

commit v2 on v1

--- a/solution.py
+++ b/solution.py
@@ -2,6 +2,7 @@
 
 import jax
 import jax.numpy as jnp
+import numpy as np
 from jax import lax
 from jax.experimental import pallas as pl
 from jax.experimental.pallas import tpu as pltpu
@@ -89,99 +90,117 @@
     return jnp.sum(folded.T, axis=0, keepdims=True)
 
 
-def qkv_kernel(count, parts, order, *refs):
-    blocks = refs[: count * parts]
-    wq, wk, wv, q_out, k_out, v_out, stat, x, w, raw, values, sem, w_sem, out_sem = refs[
-        count * parts :
-    ]
-    depth = x.shape[2]
-    rows = x.shape[1]
-    piece = rows // parts
-
-    def weight_copy(which, source):
-        return pltpu.make_async_copy(source, w.at[which], w_sem.at[which])
+def qkv_kernel(places, full_count, far_count, carried, last, order, *refs):
+    refs = list(refs)
+    blocks = [refs.pop(0) for _ in range(full_count)]
+    far = [refs.pop(0) for _ in range(far_count)]
+    sources = [refs.pop(0) for _ in range(3)]
+    before = refs.pop(0) if carried else None
+    outs = [refs.pop(0) for _ in range(3)] if last else [refs.pop(0)]
+    stat = refs.pop(0) if last else None
+    x, w, raw, values, sem, w_sem, out_sem = refs
+    count, rows, depth = x.shape
+    tile = 256
+    piece = rows // 2
+
+    def weight_copy(at, which):
+        span = pl.ds(pl.multiple_of(order[places[at]] * depth, depth), depth)
+        return pltpu.make_async_copy(sources[which].at[span], w.at[which, at], w_sem.at[which])
+
+    def weight_wait(which):
+        pltpu.make_async_copy(w.at[which], w.at[which], w_sem.at[which]).wait()
+
+    def carry(which):
+        return pltpu.make_async_copy(before.at[which], raw.at[which], w_sem.at[3 + which])
 
     def part_copy(at, part):
-        return pltpu.make_async_copy(
-            blocks[at * parts + part], x.at[at, pl.ds(part * piece, piece)], sem.at[part]
-        )
+        here = pl.ds(part * piece, piece)
+        source = blocks[at].at[here] if at < full_count else far[part]
+        return pltpu.make_async_copy(source, x.at[at, here], sem.at[part])
 
     def part_wait(part):
         whole = x.at[:, pl.ds(part * piece, piece)]
         pltpu.make_async_copy(whole, whole, sem.at[part]).wait()
 
-    weight_copy(0, wq).start()
+    for which in range(3):
+        for at in range(count):
+            weight_copy(at, which).start()
+        if which == 0:
+            for at in range(count):
+                part_copy(at, 0).start()
+        if carried:
+            carry(which).start()
     for at in range(count):
-        part_copy(at, 0).start()
-    weight_copy(1, wk).start()
-    weight_copy(2, wv).start()
-    for part in range(1, parts):
-        for at in range(count):
-            part_copy(at, part).start()
-    tile = 256
+        part_copy(at, 1).start()
     ready = 0
     leaving = []
     for start in range(0, rows, tile):
         here = slice(start, start + tile)
         needed = -(-(start + tile) // piece)
-        for which, source in enumerate((wq, wk, wv)):
+        for which in range(3):
             if start == 0:
-                weight_copy(which, source).wait()
+                weight_wait(which)
+                if carried:
+                    carry(which).wait()
             for part in range(ready, needed):
                 part_wait(part)
             ready = needed
-            total = None
+            total = raw[which, here, :] if carried else None
             for at in range(count):
-                span = pl.ds(pl.multiple_of(order[at] * depth, depth), depth)
-                term = jnp.dot(x[at, here, :], w[which, span, :], preferred_element_type=F32)
+                term = jnp.dot(x[at, here, :], w[which, at], preferred_element_type=F32)
                 total = term if total is None else total + term
-            if which < 2:
+            span = pl.ds(start, tile)
+            if last and which == 2:
+                values[here, :] = total.astype(BF16)
+                held, out = values.at[span], outs[2].at[span]
+            else:
                 raw[which, here, :] = total
+                held = raw.at[which, span]
+                out = outs[which].at[span] if last else outs[0].at[which, span]
+            if last and which < 2:
                 stat[which : which + 1, here] = row_sums(total)
-                held, out = raw.at[which], (q_out, k_out)[which]
-            else:
-                values[here, :] = total.astype(BF16)
-                held, out = values, v_out
-            span = pl.ds(start, tile)
-            leaving.append(
-                pltpu.make_async_copy(
-                    held.at[span], out.at[span], out_sem.at[which, start // tile]
-                )
-            )
+            leaving.append(pltpu.make_async_copy(held, out, out_sem.at[which, start // tile]))
             leaving[-1].start()
     for copy in leaving:
         copy.wait()
 
 
-def qkv(order, blocks, wq, wk, wv):
-    count = len(blocks)
-    parts = len(blocks[0])
-    piece, depth = blocks[0][0].shape
-    rows = piece * parts
-    columns = wq.shape[1]
-    return pl.pallas_call(
-        functools.partial(qkv_kernel, count, parts),
-        out_shape=(
-            jax.ShapeDtypeStruct((rows, columns), F32),
-            jax.ShapeDtypeStruct((rows, columns), F32),
+def qkv(order, places, blocks, far, weights, before=None, last=True):
+    count = len(places)
+    rows, depth = blocks[0].shape
+    columns = weights[0].shape[1]
+    wide = jax.ShapeDtypeStruct((rows, columns), F32)
+    if last:
+        shapes = (
+            wide,
+            wide,
             jax.ShapeDtypeStruct((rows, columns), BF16),
             jax.ShapeDtypeStruct((2, rows), F32),
-        ),
-        in_specs=[SMEM_SPEC] + [HBM_SPEC] * (count * parts + 3),
-        out_specs=(HBM_SPEC, HBM_SPEC, HBM_SPEC, VMEM_SPEC),
+        )
+        specs = (HBM_SPEC, HBM_SPEC, HBM_SPEC, VMEM_SPEC)
+    else:
+        shapes = jax.ShapeDtypeStruct((3, rows, columns), F32)
+        specs = HBM_SPEC
+    carried = [] if before is None else [before]
+    operands = [*blocks, *far, *weights, *carried]
+    return pl.pallas_call(
+        functools.partial(qkv_kernel, places, len(blocks), len(far), bool(carried), last),
+        out_shape=shapes,
+        in_specs=[SMEM_SPEC] + [HBM_SPEC] * len(operands),
+        out_specs=specs,
         scratch_shapes=[
             pltpu.VMEM((count, rows, depth), BF16),
-            pltpu.VMEM((3, wq.shape[0], columns), BF16),
-            pltpu.VMEM((2, rows, columns), F32),
+            pltpu.VMEM((3, count, depth, columns), BF16),
+            pltpu.VMEM((3, rows, columns), F32),
             pltpu.VMEM((rows, columns), BF16),
-            pltpu.SemaphoreType.DMA((parts,)),
-            pltpu.SemaphoreType.DMA((3,)),
+            pltpu.SemaphoreType.DMA((2,)),
+            pltpu.SemaphoreType.DMA((6,)),
             pltpu.SemaphoreType.DMA((3, rows // 256)),
         ],
         compiler_params=params(62),
         cost_estimate=cost(2 * rows * depth * count * 3 * columns, 9 << 20),
-        name="qkv",
-    )(order, *[piece for block in blocks for piece in block], wq, wk, wv)
+        name="qkv_last" if last else "qkv_early",
+    )(order, *operands)
 
 
 def down_rows(line):
@@ -460,25 +479,21 @@
     )(order, heads, *blocks, near_half, far_half)
 
 
-def ring_gather(block, size, parts):
+def ring_gather(block, size):
     right = [(i, (i + 1) % size) for i in range(size)]
     left = [(i, (i - 1) % size) for i in range(size)]
-    piece = block.shape[0] // parts
-    pieces = [block[at * piece : (at + 1) * piece] for at in range(parts)]
-    found = [pieces]
-    forward, backward = list(pieces), list(pieces)
+    found = [block]
+    forward = backward = block
     for _ in range((size - 1) // 2):
-        for at in range(parts):
-            forward[at] = lax.ppermute(forward[at], "tp", right)
-            backward[at] = lax.ppermute(backward[at], "tp", left)
-        found += [list(forward), list(backward)]
+        forward = lax.ppermute(forward, "tp", right)
+        backward = lax.ppermute(backward, "tp", left)
+        found += [forward, backward]
+    half = block.shape[0] // 2
     far = [
-        lax.ppermute(forward[at], "tp", right)
-        if at < parts // 2
-        else lax.ppermute(backward[at], "tp", left)
-        for at in range(parts)
+        lax.ppermute(forward[:half], "tp", right),
+        lax.ppermute(backward[half:], "tp", left),
     ]
-    return found + [far]
+    return found, far
 
 
 def ring_order(size):
@@ -533,8 +548,8 @@
     local = jnp.where(valid, page_table % pool_dev, 0)
     chosen = jnp.sum(jnp.where(source == owner, local, 0), 1)
     half = HEAD_DIM // 2
-    freqs = jnp.power(jnp.float32(ROPE_BASE), -jnp.arange(half, dtype=F32) * 2.0 / HEAD_DIM)
-    freqs = jnp.concatenate([freqs, freqs])[None]
+    freqs = np.power(np.float32(ROPE_BASE), -np.arange(half, dtype=np.float32) * 2.0 / HEAD_DIM)
+    freqs = jnp.asarray(np.concatenate([freqs, freqs])[None].astype(np.float32))
     outgoing, cosine, sine = pick_pages(
         block_len, chosen, owner[None], cache_len, freqs, key_pool, value_pool
     )
@@ -547,12 +562,17 @@
         return lax.ppermute(value, axes, pairs)
 
     order = ring_order(size)
-    blocks = ring_gather(after(flat, outgoing), size, 2)
+    blocks, far = ring_gather(after(flat, outgoing), size)
     o_1 = move(o_weight, onward)
-    o_1 = after(o_1, *(piece for block in blocks[-3:] for piece in block))
+    weights = (q_weight, k_weight, v_weight)
+    known = size - 3
+    sums = qkv(order, tuple(range(known)), blocks[:known], [], weights, last=False)
+    o_1 = after(o_1, blocks[-1], blocks[-2])
     o_2 = move(o_1, onward)
     s_1 = move(o_1, swap)
-    q_proj, k_proj, new_values, stat = qkv(order, blocks, q_weight, k_weight, v_weight)
+    q_proj, k_proj, new_values, stat = qkv(
+        order, tuple(range(known, size)), blocks[known:], far, weights, before=sums
+    )
     stat = lax.psum(stat, "tp")
     o_2 = after(o_2, stat)
     o_3 = move(o_2, onward)
@@ -579,7 +599,7 @@
     s_4 = move(o_4, swap)
     heads = lax.all_to_all(attended, "tp", split_axis=0, concat_axis=0, tiled=True)
 
-    me = lax.axis_index("tp")
+    me = after(lax.axis_index("tp"), s_1, s_2, s_3, s_4)
     turn = 1 - 2 * core
     steps = [0]
     for step in range(1, (size - 1) // 2 + 1):

time: 178 us -> 198 us (1.11)
  waiting for transfers between devices: 65.8 us -> 87.6 us
  Pallas kernels: 36.4 us -> 40.2 us
  starting transfers between devices: 53.7 us -> 51 us
    ppermute x14 -> x8, waiting for transfers between devices: 28.5 us -> 44.9 us  [the longest x3 28 us: ring_gather(): backward = lax.ppermute(backward, 'tp', left)]
    ppermute x14 -> x8, starting transfers between devices: 18.2 us -> 14.2 us  [the longest x3 12.7 us: ring_gather(): backward = lax.ppermute(backward, 'tp', left)]
    pallas_call x1 -> x2, Pallas kernels: 7.88 us -> 11.7 us  [qkv(): pl.pallas_call(functools.partial(qkv_kernel, places, len(blocks), len(far...]
    ppermute x8, waiting for transfers between devices: 10.1 us -> 13.2 us  [move(): return lax.ppermute(value, axes, pairs)]
    ppermute x8, starting transfers between devices: 18.8 us -> 21.2 us  [move(): return lax.ppermute(value, axes, pairs)]
    all_to_all x1, waiting for transfers between devices: 12.2 us -> 14.4 us  [body(): lax.all_to_all(attended, 'tp', split_axis=0, concat_axis=0, tiled=True)]
  transfers between devices with their start and end apart: 25 -> 19, of which waited for: 12 -> 8; matrix products, arithmetic and copies ran while one was open for 1% -> 1% of each run, Pallas kernels for 14% -> 14%
where the time goes in v2:
time: 198 us; the launch traced here: 197 us
  waiting for transfers between devices  87.6 us (44%)
  starting transfers between devices  51 us (26%)
  Pallas kernels  40.2 us (20%)
  blocking collectives  12.5 us (6%)
  other arithmetic  3.5 us (2%)
    ppermute x3, waiting for transfers between devices, ring_gather(): backward = lax.ppermute(backward, 'tp', left)  28 us
    ppermute x8, starting transfers between devices, move(): return lax.ppermute(value, axes, pairs)  21.2 us
    pallas_call x1, Pallas kernels, attend(): pl.pallas_call(functools.partial(attend_kernel, full), out_shape=(shape,...  16.5 us
    all_to_all x1, waiting for transfers between devices, body(): lax.all_to_all(normed, 'tp', split_axis=0, concat_axis=0, tiled=True)  15 us
    all_to_all x1, waiting for transfers between devices, body(): lax.all_to_all(attended, 'tp', split_axis=0, concat_axis=0, tiled=True)  14.4 us
    ppermute x8, waiting for transfers between devices, move(): return lax.ppermute(value, axes, pairs)  13.2 us
    ppermute x3, starting transfers between devices, ring_gather(): backward = lax.ppermute(backward, 'tp', left)  12.7 us
    psum x1, blocking collectives, body(): stat = lax.psum(stat, 'tp')  12.5 us
  transfers between devices with their start and end apart: 19, of which 8 were waited for; matrix products, arithmetic and copies ran while one was open for 1% of the time, Pallas kernels for 14%

profile of v2, /device:TPU:1, one launch (start us, length us, event | category | flops | bytes accessed | tf_op | source)
XLA Modules:
  0.0 197.3 jit_solution(13679934550460313874)
XLA Ops:
  2.0 6.5 %pick_pages.1 = (bf16[32,256,256]{2,1,0:T(8,128)(2,1)}, f32[768,128]{1,0:T(8,128)}, f32[768,128]{1,0:T(8,128)}) custom-call(s32[32]{0:T(128)} %fusion.6.chosen, s32[1]{0:T(128)} %bitcast.1.place, s32[32]{0:T(128)} %lengths.3, f32[1,128]{1,0:T(1,128)} %constant.80.clone.freqs, bf16[32,128,256]{2,1,0:T(8,128)(2,1)} %key_pool.1, bf16[32,128,256]{2,1,0:T(8,128)(2,1)} %value_pool.1), custom_call_target="tpu_custom_call" | custom-call | tf_op jit(solution)/shard_map/pick_pages/pallas_call | solution.py:67
  8.5 8.6 %all-to-all-start = ((bf16[32,256,256]{2,1,0:T(8,128)(2,1)}), bf16[32,256,256]{2,1,0:T(8,128)(2,1)}, u32[]{:S(2)}, u32[]{:S(2)}) async-start(bf16[32,256,256]{2,1,0:T(8,128)(2,1)} %get-tuple-element.16), calls=%async_computation | async-start | bytes 8388608 | tf_op jit(solution)/shard_map/all_to_all | solution.py:556
  17.2 5.7 %collective-permute-start.1 = (bf16[768,256]{1,0:T(8,128)(2,1)S(1)}, bf16[768,256]{1,0:T(8,128)(2,1)S(1)}, u32[]{:S(2)}, u32[]{:S(2)}) collective-permute-start(bf16[768,256]{1,0:T(8,128)(2,1)S(1)} %bitcast.16), channel_id=1, source_target_pairs={{0,7},{1,0},{2,1},{3,2},{4,3},{5,4},{6,5},{7,6},{8,15},{9,8},{10,9... | collective-permute-start | bytes 1179656 | tf_op jit(solution)/shard_map/ppermute | solution.py:489
  22.8 2.7 %collective-permute-start = (bf16[256,2048]{1,0:T(8,128)(2,1)S(1)}, bf16[256,2048]{1,0:T(8,128)(2,1)S(1)}, u32[]{:S(2)}, u32[]{:S(2)}) collective-permute-start(bf16[256,2048]{1,0:T(8,128)(2,1)S(1)} %copy-done.4), channel_id=1, source_target_pairs={{0,1},{1,2},{2,3},{3,4},{4,5},{5,6},{6,7},{7,0},{8,15},{9,8},{10,9... | collective-permute-start | bytes 3145736 | tf_op jit(solution)/shard_map/ppermute | solution.py:562
  25.5 5.5 %collective-permute-done.1.refs_2_ = bf16[768,256]{1,0:T(8,128)(2,1)S(1)} collective-permute-done((bf16[768,256]{1,0:T(8,128)(2,1)S(1)}, bf16[768,256]{1,0:T(8,128)(2,1)S(1)}, u32[]{:S(2)}, u32[]{:S(2)}) %collective-permute-start.1) | collective-permute-done | bytes 393248 | tf_op jit(solution)/shard_map/ppermute | solution.py:489
  31.0 3.5 %collective-permute-start.2 = (bf16[768,256]{1,0:T(8,128)(2,1)S(1)}, bf16[768,256]{1,0:T(8,128)(2,1)S(1)}, u32[]{:S(2)}, u32[]{:S(2)}) collective-permute-start(bf16[768,256]{1,0:T(8,128)(2,1)S(1)} %collective-permute-done.1.refs_2_), channel_id=1, source_target_pairs={{0,7},{1,0},{2,1},{3,2},{4,3},{5,4},{6,5},{7,6},{8,15},{9,8},{10,9... | collective-permute-start | bytes 1179656 | tf_op jit(solution)/shard_map/ppermute | solution.py:489
  34.5 17.8 %collective-permute-done.2.refs_4_ = bf16[768,256]{1,0:T(8,128)(2,1)S(1)} collective-permute-done((bf16[768,256]{1,0:T(8,128)(2,1)S(1)}, bf16[768,256]{1,0:T(8,128)(2,1)S(1)}, u32[]{:S(2)}, u32[]{:S(2)}) %collective-permute-start.2) | collective-permute-done | bytes 393248 | tf_op jit(solution)/shard_map/ppermute | solution.py:489
  52.3 3.5 %collective-permute-start.3 = (bf16[768,256]{1,0:T(8,128)(2,1)S(1)}, bf16[768,256]{1,0:T(8,128)(2,1)S(1)}, u32[]{:S(2)}, u32[]{:S(2)}) collective-permute-start(bf16[768,256]{1,0:T(8,128)(2,1)S(1)} %collective-permute-done.2.refs_4_), channel_id=1, source_target_pairs={{0,7},{1,0},{2,1},{3,2},{4,3},{5,4},{6,5},{7,6},{8,15},{9,8},{10,9... | collective-permute-start | bytes 1179656 | tf_op jit(solution)/shard_map/ppermute | solution.py:489
  55.9 4.7 %collective-permute-done.3.refs_1_ = bf16[768,256]{1,0:T(8,128)(2,1)S(1)} collective-permute-done((bf16[768,256]{1,0:T(8,128)(2,1)S(1)}, bf16[768,256]{1,0:T(8,128)(2,1)S(1)}, u32[]{:S(2)}, u32[]{:S(2)}) %collective-permute-start.3) | collective-permute-done | bytes 393248 | tf_op jit(solution)/shard_map/ppermute | solution.py:489
  60.6 7.3 %collective-permute-done.6.refs_0_ = bf16[768,256]{1,0:T(8,128)(2,1)S(1)} collective-permute-done((bf16[768,256]{1,0:T(8,128)(2,1)S(1)}, bf16[768,256]{1,0:T(8,128)(2,1)S(1)}, u32[]{:S(2)}, u32[]{:S(2)}) %collective-permute-start.6) | collective-permute-done | bytes 393248 | tf_op jit(solution)/shard_map/ppermute | solution.py:488
  70.9 5.8 %qkv_early.1.refs_7_ = f32[3,768,256]{2,1,0:T(8,128)} custom-call(s32[8]{0:T(128)} %and_select_fusion.1.order, bf16[768,256]{1,0:T(8,128)(2,1)} %bitcast.15, bf16[768,256]{1,0:T(8,128)(2,1)} %copy-done.10, bf16[768,256]{1,0:T(8,128)(2,1)} %copy-done.9, bf16[768,256]{1,0:T(8,128)(2,1)} %copy-done.12, bf16[768,256]{1,0:T(8,128)(2,1)} %copy-done.11, ...), custom_call_target="tpu_custom_call" | custom-call | flops 1509949440 | bytes 9437184 | tf_op jit(solution)/shard_map/qkv_early/pallas_call | solution.py:186
  76.7 9.6 %collective-permute-done.10.refs_3_ = bf16[384,256]{1,0:T(8,128)(2,1)} collective-permute-done((bf16[384,256]{1,0:T(8,128)(2,1)S(1)}, bf16[384,256]{1,0:T(8,128)(2,1)}, u32[]{:S(2)}, u32[]{:S(2)}) %collective-permute-start.10) | collective-permute-done | bytes 196640 | tf_op jit(solution)/shard_map/ppermute | solution.py:494
  86.2 5.9 %qkv_last.1 = (f32[768,256]{1,0:T(8,128)}, f32[768,256]{1,0:T(8,128)}, bf16[768,256]{1,0:T(8,128)(2,1)}, f32[2,768]{1,0:T(2,128)}) custom-call(s32[8]{0:T(128)} %and_select_fusion.1.order, bf16[768,256]{1,0:T(8,128)(2,1)} %copy-done.7, bf16[768,256]{1,0:T(8,128)(2,1)} %copy-done.6, bf16[384,256]{1,0:T(8,128)(2,1)} %collective-permute-done.9.refs_2_, ...), custom_call_target="tpu_custom_call" | custom-call | flops 905969664 | bytes 9437184 | tf_op jit(solution)/shard_map/qkv_last/pallas_call | solution.py:186
  92.2 12.5 %psum.7.stat = f32[2,768]{1,0:T(2,128)} all-reduce(f32[2,768]{1,0:T(2,128)} %get-tuple-element.19), channel_id=1, replica_groups=mesh['req'=32,'tp'=8] {'tp'}, use_global_device_ids=true, to_apply=%region_1.2 | all-reduce | flops 1536 | bytes 12288 | tf_op jit(solution)/shard_map/psum | solution.py:576
  105.6 13.2 %collective-permute-done.12.refs_6_ = bf16[256,2048]{1,0:T(8,128)(2,1)S(1)} collective-permute-done((bf16[256,2048]{1,0:T(8,128)(2,1)}, bf16[256,2048]{1,0:T(8,128)(2,1)S(1)}, u32[]{:S(2)}, u32[]{:S(2)}) %collective-permute-start.12) | collective-permute-done | bytes 1048608 | tf_op jit(solution)/shard_map/ppermute | solution.py:562
  118.9 1.9 collective-permute-start.14
  120.8 6.0 %collective-permute-start.7 = (bf16[256,2048]{1,0:T(8,128)(2,1)}, bf16[256,2048]{1,0:T(8,128)(2,1)}, u32[]{:S(2)}, u32[]{:S(2)}) collective-permute-start(bf16[256,2048]{1,0:T(8,128)(2,1)} %copy-done.5), channel_id=1, source_target_pairs={{0,8},{1,9},{2,10},{3,11},{4,12},{5,13},{6,14},{7,15},{8,0},{9,1},... | collective-permute-start | bytes 3145736 | tf_op jit(solution)/shard_map/ppermute | solution.py:562
  127.4 9.1 %collective-permute-start.15 = (bf16[128,2048]{1,0:T(8,128)(2,1)S(1)}, bf16[128,2048]{1,0:T(8,128)(2,1)}, u32[]{:S(2)}, u32[]{:S(2)}) collective-permute-start(bf16[128,2048]{1,0:T(8,128)(2,1)S(1)} %collective-permute-done.14.refs_8_), channel_id=1, source_target_pairs={{0,8},{1,9},{2,10},{3,11},{4,12},{5,13},{6,14},{7,15},{8,0},{9,1},... | collective-permute-start | bytes 1572872 | tf_op jit(solution)/shard_map/ppermute | solution.py:562
  136.5 16.5 %attend.1 = (bf16[768,256]{1,0:T(8,128)(2,1)}, bf16[768,256]{1,0:T(8,128)(2,1)}) custom-call(s32[1]{0:T(128)} %bitcast.1.place, s32[32]{0:T(128)} %lengths.3, s32[32,32]{1,0:T(8,128)} %page_table.1, f32[2,768]{1,0:T(2,128)} %psum.7.stat, bf16[256]{0:T(256)(128)(2,1)} %q_gain.1, bf16[256]{0:T(256)(128)(2,1)} %k_gain.1, f32[768,256]{1,0:T(8,128)} %get-tuple-element.22.q_hbm, ...), custom_call_target="tpu_custom_call" | custom-call | flops 3825205248 | bytes 9437184 | tf_op jit(solution)/shard_map/attend/pallas_call | solution.py:396
  152.9 3.5 %all-to-all-start.1 = ((bf16[8,96,256]{2,1,0:T(8,128)(2,1)}), bf16[8,96,256]{2,1,0:T(8,128)(2,1)S(1)}, u32[]{:S(2)}, u32[]{:S(2)}) async-start(bf16[8,96,256]{2,1,0:T(8,128)(2,1)} %bitcast.18), calls=%async_computation.1 | async-start | bytes 786432 | tf_op jit(solution)/shard_map/all_to_all | solution.py:600
  157.1 14.4 %all-to-all-done.1 = bf16[8,96,256]{2,1,0:T(8,128)(2,1)S(1)} async-done(((bf16[8,96,256]{2,1,0:T(8,128)(2,1)}), bf16[8,96,256]{2,1,0:T(8,128)(2,1)S(1)}, u32[]{:S(2)}, u32[]{:S(2)}) %all-to-all-start.1) | async-done | bytes 393248 | tf_op jit(solution)/shard_map/all_to_all | solution.py:600
  172.3 5.5 %project.1 = bf16[768,256]{1,0:T(8,128)(2,1)} custom-call(s32[9]{0:T(128)} %pad_add_fusion.order, bf16[768,256]{1,0:T(8,128)(2,1)} %bitcast.12, bf16[256,2048]{1,0:T(8,128)(2,1)} %refs_1_.1, bf16[256,2048]{1,0:T(8,128)(2,1)} %copy-done.5, bf16[256,2048]{1,0:T(8,128)(2,1)} %collective-permute-done.7.refs_3_, ...), custom_call_target="tpu_custom_call" | custom-call | flops 805306368 | bytes 9437184 | tf_op jit(solution)/shard_map/project/pallas_call | solution.py:465
  177.9 3.5 %all-to-all-start.2 = ((bf16[8,96,256]{2,1,0:T(8,128)(2,1)}), bf16[8,96,256]{2,1,0:T(8,128)(2,1)S(1)}, u32[]{:S(2)}, u32[]{:S(2)}) async-start(bf16[8,96,256]{2,1,0:T(8,128)(2,1)} %bitcast.13), calls=%async_computation.2 | async-start | bytes 786432 | tf_op jit(solution)/shard_map/all_to_all | solution.py:611
  181.4 15.0 %all-to-all-done.2 = bf16[8,96,256]{2,1,0:T(8,128)(2,1)S(1)} async-done(((bf16[8,96,256]{2,1,0:T(8,128)(2,1)}), bf16[8,96,256]{2,1,0:T(8,128)(2,1)S(1)}, u32[]{:S(2)}, u32[]{:S(2)}) %all-to-all-start.2) | async-done | bytes 393248 | tf_op jit(solution)/shard_map/all_to_all | solution.py:611
  (61 shorter events, 8.2 us)
Async XLA Ops:
  8.5 61.8 %copy-start.13 = (s32[8]{0:T(128)S(1)}, s32[8]{0:T(128)}, u32[]{:S(2)}) copy-start(s32[8]{0:T(128)} %constant.81.clone) | copy-start | bytes 100
  8.5 127.9 %all-to-all-start = ((bf16[32,256,256]{2,1,0:T(8,128)(2,1)}), bf16[32,256,256]{2,1,0:T(8,128)(2,1)}, u32[]{:S(2)}, u32[]{:S(2)}) async-start(bf16[32,256,256]{2,1,0:T(8,128)(2,1)} %get-tuple-element.16), calls=%async_computation | async-start | bytes 8388608 | tf_op jit(solution)/shard_map/all_to_all | solution.py:556
  17.2 13.8 %collective-permute-start.1 = (bf16[768,256]{1,0:T(8,128)(2,1)S(1)}, bf16[768,256]{1,0:T(8,128)(2,1)S(1)}, u32[]{:S(2)}, u32[]{:S(2)}) collective-permute-start(bf16[768,256]{1,0:T(8,128)(2,1)S(1)} %bitcast.16), channel_id=1, source_target_pairs={{0,7},{1,0},{2,1},{3,2},{4,3},{5,4},{6,5},{7,6},{8,15},{9,8},{10,9... | collective-permute-start | bytes 1179656 | tf_op jit(solution)/shard_map/ppermute | solution.py:489
  22.8 11.7 %collective-permute-start.4 = (bf16[768,256]{1,0:T(8,128)(2,1)S(1)}, bf16[768,256]{1,0:T(8,128)(2,1)S(1)}, u32[]{:S(2)}, u32[]{:S(2)}) collective-permute-start(bf16[768,256]{1,0:T(8,128)(2,1)S(1)} %bitcast.17), channel_id=1, source_target_pairs={{0,1},{1,2},{2,3},{3,4},{4,5},{5,6},{6,7},{7,0},{8,9},{9,10},{10,1... | collective-permute-start | bytes 1179656 | tf_op jit(solution)/shard_map/ppermute | solution.py:488
  22.8 33.0 %collective-permute-start = (bf16[256,2048]{1,0:T(8,128)(2,1)S(1)}, bf16[256,2048]{1,0:T(8,128)(2,1)S(1)}, u32[]{:S(2)}, u32[]{:S(2)}) collective-permute-start(bf16[256,2048]{1,0:T(8,128)(2,1)S(1)} %copy-done.4), channel_id=1, source_target_pairs={{0,1},{1,2},{2,3},{3,4},{4,5},{5,6},{6,7},{7,0},{8,15},{9,8},{10,9... | collective-permute-start | bytes 3145736 | tf_op jit(solution)/shard_map/ppermute | solution.py:562
  31.0 36.9 %copy-start.9 = (bf16[768,256]{1,0:T(8,128)(2,1)}, bf16[768,256]{1,0:T(8,128)(2,1)S(1)}, u32[]{:S(2)}) copy-start(bf16[768,256]{1,0:T(8,128)(2,1)S(1)} %collective-permute-done.1.refs_2_) | copy-start | bytes 1179652
  31.0 21.3 %collective-permute-start.2 = (bf16[768,256]{1,0:T(8,128)(2,1)S(1)}, bf16[768,256]{1,0:T(8,128)(2,1)S(1)}, u32[]{:S(2)}, u32[]{:S(2)}) collective-permute-start(bf16[768,256]{1,0:T(8,128)(2,1)S(1)} %collective-permute-done.1.refs_2_), channel_id=1, source_target_pairs={{0,7},{1,0},{2,1},{3,2},{4,3},{5,4},{6,5},{7,6},{8,15},{9,8},{10,9... | collective-permute-start | bytes 1179656 | tf_op jit(solution)/shard_map/ppermute | solution.py:489
  34.5 33.4 %copy-start.10 = (bf16[768,256]{1,0:T(8,128)(2,1)}, bf16[768,256]{1,0:T(8,128)(2,1)S(1)}, u32[]{:S(2)}) copy-start(bf16[768,256]{1,0:T(8,128)(2,1)S(1)} %collective-permute-done.4.refs_1_) | copy-start | bytes 1179652
  34.5 21.3 %collective-permute-start.5 = (bf16[768,256]{1,0:T(8,128)(2,1)S(1)}, bf16[768,256]{1,0:T(8,128)(2,1)S(1)}, u32[]{:S(2)}, u32[]{:S(2)}) collective-permute-start(bf16[768,256]{1,0:T(8,128)(2,1)S(1)} %collective-permute-done.4.refs_1_), channel_id=1, source_target_pairs={{0,1},{1,2},{2,3},{3,4},{4,5},{5,6},{6,7},{7,0},{8,9},{9,10},{10,1... | collective-permute-start | bytes 1179656 | tf_op jit(solution)/shard_map/ppermute | solution.py:488
  52.3 8.2 %collective-permute-start.3 = (bf16[768,256]{1,0:T(8,128)(2,1)S(1)}, bf16[768,256]{1,0:T(8,128)(2,1)S(1)}, u32[]{:S(2)}, u32[]{:S(2)}) collective-permute-start(bf16[768,256]{1,0:T(8,128)(2,1)S(1)} %collective-permute-done.2.refs_4_), channel_id=1, source_target_pairs={{0,7},{1,0},{2,1},{3,2},{4,3},{5,4},{6,5},{7,6},{8,15},{9,8},{10,9... | collective-permute-start | bytes 1179656 | tf_op jit(solution)/shard_map/ppermute | solution.py:489
  55.9 12.0 %collective-permute-start.6 = (bf16[768,256]{1,0:T(8,128)(2,1)S(1)}, bf16[768,256]{1,0:T(8,128)(2,1)S(1)}, u32[]{:S(2)}, u32[]{:S(2)}) collective-permute-start(bf16[768,256]{1,0:T(8,128)(2,1)S(1)} %collective-permute-done.5.refs_3_), channel_id=1, source_target_pairs={{0,1},{1,2},{2,3},{3,4},{4,5},{5,6},{6,7},{7,0},{8,9},{9,10},{10,1... | collective-permute-start | bytes 1179656 | tf_op jit(solution)/shard_map/ppermute | solution.py:488
  67.9 36.8 %collective-permute-start.8 = (bf16[256,2048]{1,0:T(8,128)(2,1)S(1)}, bf16[256,2048]{1,0:T(8,128)(2,1)}, u32[]{:S(2)}, u32[]{:S(2)}) collective-permute-start(bf16[256,2048]{1,0:T(8,128)(2,1)S(1)} %collective-permute-done.refs_2_), channel_id=1, source_target_pairs={{0,1},{1,2},{2,3},{3,4},{4,5},{5,6},{6,7},{7,0},{8,15},{9,8},{10,9... | collective-permute-start | bytes 3145736 | tf_op jit(solution)/shard_map/ppermute | solution.py:562
  68.0 18.2 %collective-permute-start.10 = (bf16[384,256]{1,0:T(8,128)(2,1)S(1)}, bf16[384,256]{1,0:T(8,128)(2,1)}, u32[]{:S(2)}, u32[]{:S(2)}) collective-permute-start(bf16[384,256]{1,0:T(8,128)(2,1)S(1)} %slice.9), channel_id=1, source_target_pairs={{0,7},{1,0},{2,1},{3,2},{4,3},{5,4},{6,5},{7,6},{8,15},{9,8},{10,9... | collective-permute-start | bytes 589832 | tf_op jit(solution)/shard_map/ppermute | solution.py:494
  68.8 17.4 %collective-permute-start.9 = (bf16[384,256]{1,0:T(8,128)(2,1)}, bf16[384,256]{1,0:T(8,128)(2,1)}, u32[]{:S(2)}, u32[]{:S(2)}) collective-permute-start(bf16[384,256]{1,0:T(8,128)(2,1)} %slice.8), channel_id=1, source_target_pairs={{0,1},{1,2},{2,3},{3,4},{4,5},{5,6},{6,7},{7,0},{8,9},{9,10},{10,1... | collective-permute-start | bytes 589832 | tf_op jit(solution)/shard_map/ppermute | solution.py:493
  104.7 14.2 %collective-permute-start.12 = (bf16[256,2048]{1,0:T(8,128)(2,1)}, bf16[256,2048]{1,0:T(8,128)(2,1)S(1)}, u32[]{:S(2)}, u32[]{:S(2)}) collective-permute-start(bf16[256,2048]{1,0:T(8,128)(2,1)} %collective-permute-done.8.refs_4_), channel_id=1, source_target_pairs={{0,1},{1,2},{2,3},{3,4},{4,5},{5,6},{6,7},{7,0},{8,15},{9,8},{10,9... | collective-permute-start | bytes 3145736 | tf_op jit(solution)/shard_map/ppermute | solution.py:562
  118.9 34.1 %copy-start = (bf16[256,2048]{1,0:T(8,128)(2,1)}, bf16[256,2048]{1,0:T(8,128)(2,1)S(1)}, u32[]{:S(2)}) copy-start(bf16[256,2048]{1,0:T(8,128)(2,1)S(1)} %collective-permute-done.12.refs_6_) | copy-start | bytes 3145732
  118.9 8.5 %collective-permute-start.14 = (bf16[128,2048]{1,0:T(8,128)(2,1)S(1)}, bf16[128,2048]{1,0:T(8,128)(2,1)S(1)}, u32[]{:S(2)}, u32[]{:S(2)}) collective-permute-start(bf16[128,2048]{1,0:T(8,128)(2,1)S(1)} %constant_dynamic-slice_fusion), channel_id=1, source_target_pairs={{0,1},{1,2},{2,3},{3,4},{4,5},{5,6},{6,7},{7,0},{8,15},{9,8},{10,9... | collective-permute-start | bytes 1572872 | tf_op jit(solution)/shard_map/ppermute | solution.py:562
  120.8 35.6 %collective-permute-start.7 = (bf16[256,2048]{1,0:T(8,128)(2,1)}, bf16[256,2048]{1,0:T(8,128)(2,1)}, u32[]{:S(2)}, u32[]{:S(2)}) collective-permute-start(bf16[256,2048]{1,0:T(8,128)(2,1)} %copy-done.5), channel_id=1, source_target_pairs={{0,8},{1,9},{2,10},{3,11},{4,12},{5,13},{6,14},{7,15},{8,0},{9,1},... | collective-permute-start | bytes 3145736 | tf_op jit(solution)/shard_map/ppermute | solution.py:562
  126.9 29.6 %collective-permute-start.11 = (bf16[256,2048]{1,0:T(8,128)(2,1)}, bf16[256,2048]{1,0:T(8,128)(2,1)}, u32[]{:S(2)}, u32[]{:S(2)}) collective-permute-start(bf16[256,2048]{1,0:T(8,128)(2,1)} %collective-permute-done.8.refs_4_), channel_id=1, source_target_pairs={{0,8},{1,9},{2,10},{3,11},{4,12},{5,13},{6,14},{7,15},{8,0},{9,1},... | collective-permute-start | bytes 3145736 | tf_op jit(solution)/shard_map/ppermute | solution.py:562
  126.9 29.6 %collective-permute-start.13 = (bf16[256,2048]{1,0:T(8,128)(2,1)S(1)}, bf16[256,2048]{1,0:T(8,128)(2,1)}, u32[]{:S(2)}, u32[]{:S(2)}) collective-permute-start(bf16[256,2048]{1,0:T(8,128)(2,1)S(1)} %collective-permute-done.12.refs_6_), channel_id=1, source_target_pairs={{0,8},{1,9},{2,10},{3,11},{4,12},{5,13},{6,14},{7,15},{8,0},{9,1},... | collective-permute-start | bytes 3145736 | tf_op jit(solution)/shard_map/ppermute | solution.py:562
  127.4 25.6 %copy-start.8 = (bf16[128,2048]{1,0:T(8,128)(2,1)}, bf16[128,2048]{1,0:T(8,128)(2,1)S(1)}, u32[]{:S(2)}) copy-start(bf16[128,2048]{1,0:T(8,128)(2,1)S(1)} %collective-permute-done.14.refs_8_) | copy-start | bytes 1572868
  127.4 29.1 %collective-permute-start.15 = (bf16[128,2048]{1,0:T(8,128)(2,1)S(1)}, bf16[128,2048]{1,0:T(8,128)(2,1)}, u32[]{:S(2)}, u32[]{:S(2)}) collective-permute-start(bf16[128,2048]{1,0:T(8,128)(2,1)S(1)} %collective-permute-done.14.refs_8_), channel_id=1, source_target_pairs={{0,8},{1,9},{2,10},{3,11},{4,12},{5,13},{6,14},{7,15},{8,0},{9,1},... | collective-permute-start | bytes 1572872 | tf_op jit(solution)/shard_map/ppermute | solution.py:562
  152.9 18.6 %all-to-all-start.1 = ((bf16[8,96,256]{2,1,0:T(8,128)(2,1)}), bf16[8,96,256]{2,1,0:T(8,128)(2,1)S(1)}, u32[]{:S(2)}, u32[]{:S(2)}) async-start(bf16[8,96,256]{2,1,0:T(8,128)(2,1)} %bitcast.18), calls=%async_computation.1 | async-start | bytes 786432 | tf_op jit(solution)/shard_map/all_to_all | solution.py:600
  177.9 18.5 %all-to-all-start.2 = ((bf16[8,96,256]{2,1,0:T(8,128)(2,1)}), bf16[8,96,256]{2,1,0:T(8,128)(2,1)S(1)}, u32[]{:S(2)}, u32[]{:S(2)}) async-start(bf16[8,96,256]{2,1,0:T(8,128)(2,1)} %bitcast.13), calls=%async_computation.2 | async-start | bytes 786432 | tf_op jit(solution)/shard_map/all_to_all | solution.py:611
  (11 other events, 150.1 us)

commit v3 on v1

--- a/solution.py
+++ b/solution.py
@@ -2,6 +2,7 @@
 
 import jax
 import jax.numpy as jnp
+import numpy as np
 from jax import lax
 from jax.experimental import pallas as pl
 from jax.experimental.pallas import tpu as pltpu
@@ -533,8 +534,8 @@
     local = jnp.where(valid, page_table % pool_dev, 0)
     chosen = jnp.sum(jnp.where(source == owner, local, 0), 1)
     half = HEAD_DIM // 2
-    freqs = jnp.power(jnp.float32(ROPE_BASE), -jnp.arange(half, dtype=F32) * 2.0 / HEAD_DIM)
-    freqs = jnp.concatenate([freqs, freqs])[None]
+    freqs = np.power(np.float32(ROPE_BASE), -np.arange(half, dtype=np.float32) * 2.0 / HEAD_DIM)
+    freqs = jnp.asarray(np.concatenate([freqs, freqs])[None].astype(np.float32))
     outgoing, cosine, sine = pick_pages(
         block_len, chosen, owner[None], cache_len, freqs, key_pool, value_pool
     )
@@ -579,7 +580,7 @@
     s_4 = move(o_4, swap)
     heads = lax.all_to_all(attended, "tp", split_axis=0, concat_axis=0, tiled=True)
 
-    me = lax.axis_index("tp")
+    me = after(lax.axis_index("tp"), s_1, s_2, s_3, s_4)
     turn = 1 - 2 * core
     steps = [0]
     for step in range(1, (size - 1) // 2 + 1):

time: 178 us -> 186 us (1.045)
  waiting for transfers between devices: 65.8 us -> 71.3 us
  starting transfers between devices: 53.7 us -> 59 us
    ppermute x8, starting transfers between devices: 18.8 us -> 24.7 us  [move(): return lax.ppermute(value, axes, pairs)]
    ppermute x8, waiting for transfers between devices: 10.1 us -> 13.1 us  [move(): return lax.ppermute(value, axes, pairs)]
    all_to_all x1, waiting for transfers between devices: 12.2 us -> 14.6 us  [body(): lax.all_to_all(attended, 'tp', split_axis=0, concat_axis=0, tiled=True)]
  transfers between devices with their start and end apart: 25 -> 25, of which waited for: 12 -> 12; matrix products, arithmetic and copies ran while one was open for 1% -> 1% of each run, Pallas kernels for 14% -> 13%
where the time goes in v3:
time: 186 us
  waiting for transfers between devices  71.3 us (38%)
  starting transfers between devices  59 us (32%)
  Pallas kernels  36.5 us (20%)
  blocking collectives  13 us (7%)
  other arithmetic  3.37 us (2%)
    ppermute x8, starting transfers between devices, move(): return lax.ppermute(value, axes, pairs)  24.7 us
    pallas_call x1, Pallas kernels, attend(): pl.pallas_call(functools.partial(attend_kernel, full), out_shape=(shape,...  16.4 us
    ppermute x6, waiting for transfers between devices, ring_gather(): backward[at] = lax.ppermute(backward[at], 'tp', left)  16.3 us
    ppermute x6, starting transfers between devices, ring_gather(): backward[at] = lax.ppermute(backward[at], 'tp', left)  15.8 us
    all_to_all x1, waiting for transfers between devices, body(): lax.all_to_all(normed, 'tp', split_axis=0, concat_axis=0, tiled=True)  15 us
    all_to_all x1, waiting for transfers between devices, body(): lax.all_to_all(attended, 'tp', split_axis=0, concat_axis=0, tiled=True)  14.6 us
    ppermute x8, waiting for transfers between devices, move(): return lax.ppermute(value, axes, pairs)  13.1 us
    psum x1, blocking collectives, body(): stat = lax.psum(stat, 'tp')  13 us
  transfers between devices with their start and end apart: 25, of which 12 were waited for; matrix products, arithmetic and copies ran while one was open for 1% of the time, Pallas kernels for 13%

profile of v3, /device:TPU:1, one launch (start us, length us, event | category | flops | bytes accessed | tf_op | source)
XLA Modules:
  0.0 185.5 jit_solution(3001720226283160604)
XLA Ops:
  2.0 6.5 %pick_pages.1 = (bf16[32,256,256]{2,1,0:T(8,128)(2,1)}, f32[768,128]{1,0:T(8,128)}, f32[768,128]{1,0:T(8,128)}) custom-call(s32[32]{0:T(128)} %fusion.6.chosen, s32[1]{0:T(128)} %bitcast.1.place, s32[32]{0:T(128)} %lengths.3, f32[1,128]{1,0:T(1,128)} %constant.80.clone.freqs, bf16[32,128,256]{2,1,0:T(8,128)(2,1)} %key_pool.1, bf16[32,128,256]{2,1,0:T(8,128)(2,1)} %value_pool.1), custom_call_target="tpu_custom_call" | custom-call | tf_op jit(solution)/shard_map/pick_pages/pallas_call | solution.py:67
  8.6 8.6 %all-to-all-start = ((bf16[32,256,256]{2,1,0:T(8,128)(2,1)}), bf16[32,256,256]{2,1,0:T(8,128)(2,1)}, u32[]{:S(2)}, u32[]{:S(2)}) async-start(bf16[32,256,256]{2,1,0:T(8,128)(2,1)} %get-tuple-element.16), calls=%async_computation | async-start | bytes 8388608 | tf_op jit(solution)/shard_map/all_to_all | solution.py:542
  17.2 5.7 %collective-permute-start = (bf16[256,2048]{1,0:T(8,128)(2,1)S(1)}, bf16[256,2048]{1,0:T(8,128)(2,1)S(1)}, u32[]{:S(2)}, u32[]{:S(2)}) collective-permute-start(bf16[256,2048]{1,0:T(8,128)(2,1)S(1)} %copy-done.3), channel_id=1, source_target_pairs={{0,1},{1,2},{2,3},{3,4},{4,5},{5,6},{6,7},{7,0},{8,15},{9,8},{10,9... | collective-permute-start | bytes 3145736 | tf_op jit(solution)/shard_map/ppermute | solution.py:548
  24.5 2.7 %collective-permute-start.7 = (bf16[384,256]{1,0:T(8,128)(2,1)S(1)}, bf16[384,256]{1,0:T(8,128)(2,1)S(1)}, u32[]{:S(2)}, u32[]{:S(2)}) collective-permute-start(bf16[384,256]{1,0:T(8,128)(2,1)S(1)} %get-tuple-element.30.refs_0_), channel_id=1, source_target_pairs={{0,7},{1,0},{2,1},{3,2},{4,3},{5,4},{6,5},{7,6},{8,15},{9,8},{10,9... | collective-permute-start | bytes 589832 | tf_op jit(solution)/shard_map/ppermute | solution.py:474
  27.2 15.9 %collective-permute-done.10.refs_5_ = bf16[384,256]{1,0:T(8,128)(2,1)S(1)} collective-permute-done((bf16[384,256]{1,0:T(8,128)(2,1)S(1)}, bf16[384,256]{1,0:T(8,128)(2,1)S(1)}, u32[]{:S(2)}, u32[]{:S(2)}) %collective-permute-start.10) | collective-permute-done | bytes 196640 | tf_op jit(solution)/shard_map/ppermute | solution.py:474
  43.1 3.5 %collective-permute-start.11 = (bf16[384,256]{1,0:T(8,128)(2,1)S(1)}, bf16[384,256]{1,0:T(8,128)(2,1)S(1)}, u32[]{:S(2)}, u32[]{:S(2)}) collective-permute-start(bf16[384,256]{1,0:T(8,128)(2,1)S(1)} %collective-permute-done.10.refs_5_), channel_id=1, source_target_pairs={{0,7},{1,0},{2,1},{3,2},{4,3},{5,4},{6,5},{7,6},{8,15},{9,8},{10,9... | collective-permute-start | bytes 589832 | tf_op jit(solution)/shard_map/ppermute | solution.py:474
  46.7 2.6 %collective-permute-start.8 = (bf16[384,256]{1,0:T(8,128)(2,1)S(1)}, bf16[384,256]{1,0:T(8,128)(2,1)S(1)}, u32[]{:S(2)}, u32[]{:S(2)}) collective-permute-start(bf16[384,256]{1,0:T(8,128)(2,1)S(1)} %collective-permute-done.7.refs_4_), channel_id=1, source_target_pairs={{0,7},{1,0},{2,1},{3,2},{4,3},{5,4},{6,5},{7,6},{8,15},{9,8},{10,9... | collective-permute-start | bytes 589832 | tf_op jit(solution)/shard_map/ppermute | solution.py:474
  49.8 3.5 %collective-permute-start.12 = (bf16[384,256]{1,0:T(8,128)(2,1)S(1)}, bf16[384,256]{1,0:T(8,128)(2,1)S(1)}, u32[]{:S(2)}, u32[]{:S(2)}) collective-permute-start(bf16[384,256]{1,0:T(8,128)(2,1)S(1)} %collective-permute-done.11.refs_9_), channel_id=1, source_target_pairs={{0,7},{1,0},{2,1},{3,2},{4,3},{5,4},{6,5},{7,6},{8,15},{9,8},{10,9... | collective-permute-start | bytes 589832 | tf_op jit(solution)/shard_map/ppermute | solution.py:474
  53.4 3.6 %collective-permute-done.5.refs_7_ = bf16[384,256]{1,0:T(8,128)(2,1)S(1)} collective-permute-done((bf16[384,256]{1,0:T(8,128)(2,1)S(1)}, bf16[384,256]{1,0:T(8,128)(2,1)S(1)}, u32[]{:S(2)}, u32[]{:S(2)}) %collective-permute-start.5) | collective-permute-done | bytes 196640 | tf_op jit(solution)/shard_map/ppermute | solution.py:473
  57.1 2.7 %collective-permute-start.9 = (bf16[384,256]{1,0:T(8,128)(2,1)S(1)}, bf16[384,256]{1,0:T(8,128)(2,1)S(1)}, u32[]{:S(2)}, u32[]{:S(2)}) collective-permute-start(bf16[384,256]{1,0:T(8,128)(2,1)S(1)} %collective-permute-done.8.refs_8_), channel_id=1, source_target_pairs={{0,7},{1,0},{2,1},{3,2},{4,3},{5,4},{6,5},{7,6},{8,15},{9,8},{10,9... | collective-permute-start | bytes 589832 | tf_op jit(solution)/shard_map/ppermute | solution.py:474
  63.8 2.8 %collective-permute-done.14.refs_15_ = bf16[384,256]{1,0:T(8,128)(2,1)S(1)} collective-permute-done((bf16[384,256]{1,0:T(8,128)(2,1)S(1)}, bf16[384,256]{1,0:T(8,128)(2,1)S(1)}, u32[]{:S(2)}, u32[]{:S(2)}) %collective-permute-start.14) | collective-permute-done | bytes 196640 | tf_op jit(solution)/shard_map/ppermute | solution.py:479
  66.6 3.2 %collective-permute-done.13.refs_14_ = bf16[384,256]{1,0:T(8,128)(2,1)S(1)} collective-permute-done((bf16[384,256]{1,0:T(8,128)(2,1)S(1)}, bf16[384,256]{1,0:T(8,128)(2,1)S(1)}, u32[]{:S(2)}, u32[]{:S(2)}) %collective-permute-start.13) | collective-permute-done | bytes 196640 | tf_op jit(solution)/shard_map/ppermute | solution.py:477
  71.0 7.9 %qkv.1 = (f32[768,256]{1,0:T(8,128)}, f32[768,256]{1,0:T(8,128)}, bf16[768,256]{1,0:T(8,128)(2,1)}, f32[2,768]{1,0:T(2,128)}) custom-call(s32[8]{0:T(128)} %and_select_fusion.1.order, bf16[384,256]{1,0:T(8,128)(2,1)} %copy-done.6, bf16[384,256]{1,0:T(8,128)(2,1)} %copy-done.5, bf16[384,256]{1,0:T(8,128)(2,1)} %copy-done.9, bf16[384,256]{1,0:T(8,128)(2,1)} %copy-done.10, ...), custom_call_target="tpu_custom_call" | custom-call | flops 2415919104 | bytes 9437184 | tf_op jit(solution)/shard_map/qkv/pallas_call | solution.py:163
  78.9 13.0 %psum.7.stat = f32[2,768]{1,0:T(2,128)} all-reduce(f32[2,768]{1,0:T(2,128)} %get-tuple-element.19), channel_id=1, replica_groups=mesh['req'=32,'tp'=8] {'tp'}, use_global_device_ids=true, to_apply=%region_1.2 | all-reduce | flops 1536 | bytes 12288 | tf_op jit(solution)/shard_map/psum | solution.py:557
  93.4 12.7 %collective-permute-done.18.refs_6_ = bf16[256,2048]{1,0:T(8,128)(2,1)S(1)} collective-permute-done((bf16[256,2048]{1,0:T(8,128)(2,1)}, bf16[256,2048]{1,0:T(8,128)(2,1)S(1)}, u32[]{:S(2)}, u32[]{:S(2)}) %collective-permute-start.18) | collective-permute-done | bytes 1048608 | tf_op jit(solution)/shard_map/ppermute | solution.py:548
  106.1 2.4 %collective-permute-start.20 = (bf16[128,2048]{1,0:T(8,128)(2,1)S(1)}, bf16[128,2048]{1,0:T(8,128)(2,1)}, u32[]{:S(2)}, u32[]{:S(2)}) collective-permute-start(bf16[128,2048]{1,0:T(8,128)(2,1)S(1)} %constant_dynamic-slice_fusion), channel_id=1, source_target_pairs={{0,1},{1,2},{2,3},{3,4},{4,5},{5,6},{6,7},{7,0},{8,15},{9,8},{10,9... | collective-permute-start | bytes 1572872 | tf_op jit(solution)/shard_map/ppermute | solution.py:548
  108.5 5.2 %collective-permute-start.15 = (bf16[256,2048]{1,0:T(8,128)(2,1)}, bf16[256,2048]{1,0:T(8,128)(2,1)}, u32[]{:S(2)}, u32[]{:S(2)}) collective-permute-start(bf16[256,2048]{1,0:T(8,128)(2,1)} %copy-done.4), channel_id=1, source_target_pairs={{0,8},{1,9},{2,10},{3,11},{4,12},{5,13},{6,14},{7,15},{8,0},{9,1},... | collective-permute-start | bytes 3145736 | tf_op jit(solution)/shard_map/ppermute | solution.py:548
  114.7 9.5 %collective-permute-start.21 = (bf16[128,2048]{1,0:T(8,128)(2,1)}, bf16[128,2048]{1,0:T(8,128)(2,1)}, u32[]{:S(2)}, u32[]{:S(2)}) collective-permute-start(bf16[128,2048]{1,0:T(8,128)(2,1)} %collective-permute-done.20.refs_8_), channel_id=1, source_target_pairs={{0,8},{1,9},{2,10},{3,11},{4,12},{5,13},{6,14},{7,15},{8,0},{9,1},... | collective-permute-start | bytes 1572872 | tf_op jit(solution)/shard_map/ppermute | solution.py:548
  124.1 16.4 %attend.1 = (bf16[768,256]{1,0:T(8,128)(2,1)}, bf16[768,256]{1,0:T(8,128)(2,1)}) custom-call(s32[1]{0:T(128)} %bitcast.1.place, s32[32]{0:T(128)} %lengths.3, s32[32,32]{1,0:T(8,128)} %page_table.1, f32[2,768]{1,0:T(2,128)} %psum.7.stat, bf16[256]{0:T(256)(128)(2,1)} %q_gain.1, bf16[256]{0:T(256)(128)(2,1)} %k_gain.1, f32[768,256]{1,0:T(8,128)} %get-tuple-element.22.q_hbm, ...), custom_call_target="tpu_custom_call" | custom-call | flops 3825205248 | bytes 9437184 | tf_op jit(solution)/shard_map/attend/pallas_call | solution.py:378
  140.6 4.0 %all-to-all-start.1 = ((bf16[8,96,256]{2,1,0:T(8,128)(2,1)}), bf16[8,96,256]{2,1,0:T(8,128)(2,1)S(1)}, u32[]{:S(2)}, u32[]{:S(2)}) async-start(bf16[8,96,256]{2,1,0:T(8,128)(2,1)} %bitcast.16), calls=%async_computation.1 | async-start | bytes 786432 | tf_op jit(solution)/shard_map/all_to_all | solution.py:581
  145.2 14.6 %all-to-all-done.1 = bf16[8,96,256]{2,1,0:T(8,128)(2,1)S(1)} async-done(((bf16[8,96,256]{2,1,0:T(8,128)(2,1)}), bf16[8,96,256]{2,1,0:T(8,128)(2,1)S(1)}, u32[]{:S(2)}, u32[]{:S(2)}) %all-to-all-start.1) | async-done | bytes 393248 | tf_op jit(solution)/shard_map/all_to_all | solution.py:581
  160.5 5.6 %project.1 = bf16[768,256]{1,0:T(8,128)(2,1)} custom-call(s32[9]{0:T(128)} %pad_add_fusion.order, bf16[768,256]{1,0:T(8,128)(2,1)} %bitcast.12, bf16[256,2048]{1,0:T(8,128)(2,1)} %refs_1_.1, bf16[256,2048]{1,0:T(8,128)(2,1)} %copy-done.4, bf16[256,2048]{1,0:T(8,128)(2,1)} %collective-permute-done.15.refs_3_, ...), custom_call_target="tpu_custom_call" | custom-call | flops 805306368 | bytes 9437184 | tf_op jit(solution)/shard_map/project/pallas_call | solution.py:447
  166.1 3.5 %all-to-all-start.2 = ((bf16[8,96,256]{2,1,0:T(8,128)(2,1)}), bf16[8,96,256]{2,1,0:T(8,128)(2,1)S(1)}, u32[]{:S(2)}, u32[]{:S(2)}) async-start(bf16[8,96,256]{2,1,0:T(8,128)(2,1)} %bitcast.13), calls=%async_computation.2 | async-start | bytes 786432 | tf_op jit(solution)/shard_map/all_to_all | solution.py:592
  169.6 15.0 %all-to-all-done.2 = bf16[8,96,256]{2,1,0:T(8,128)(2,1)S(1)} async-done(((bf16[8,96,256]{2,1,0:T(8,128)(2,1)}), bf16[8,96,256]{2,1,0:T(8,128)(2,1)S(1)}, u32[]{:S(2)}, u32[]{:S(2)}) %all-to-all-start.2) | async-done | bytes 393248 | tf_op jit(solution)/shard_map/all_to_all | solution.py:592
  (85 shorter events, 13.4 us)
Async XLA Ops:
  8.6 115.5 %all-to-all-start = ((bf16[32,256,256]{2,1,0:T(8,128)(2,1)}), bf16[32,256,256]{2,1,0:T(8,128)(2,1)}, u32[]{:S(2)}, u32[]{:S(2)}) async-start(bf16[32,256,256]{2,1,0:T(8,128)(2,1)} %get-tuple-element.16), calls=%async_computation | async-start | bytes 8388608 | tf_op jit(solution)/shard_map/all_to_all | solution.py:542
  17.2 52.5 %collective-permute-start = (bf16[256,2048]{1,0:T(8,128)(2,1)S(1)}, bf16[256,2048]{1,0:T(8,128)(2,1)S(1)}, u32[]{:S(2)}, u32[]{:S(2)}) collective-permute-start(bf16[256,2048]{1,0:T(8,128)(2,1)S(1)} %copy-done.3), channel_id=1, source_target_pairs={{0,1},{1,2},{2,3},{3,4},{4,5},{5,6},{6,7},{7,0},{8,15},{9,8},{10,9... | collective-permute-start | bytes 3145736 | tf_op jit(solution)/shard_map/ppermute | solution.py:548
  23.0 20.1 %collective-permute-start.10 = (bf16[384,256]{1,0:T(8,128)(2,1)S(1)}, bf16[384,256]{1,0:T(8,128)(2,1)S(1)}, u32[]{:S(2)}, u32[]{:S(2)}) collective-permute-start(bf16[384,256]{1,0:T(8,128)(2,1)S(1)} %get-tuple-element.29.refs_1_), channel_id=1, source_target_pairs={{0,7},{1,0},{2,1},{3,2},{4,3},{5,4},{6,5},{7,6},{8,15},{9,8},{10,9... | collective-permute-start | bytes 589832 | tf_op jit(solution)/shard_map/ppermute | solution.py:474
  23.8 22.8 %collective-permute-start.1 = (bf16[384,256]{1,0:T(8,128)(2,1)S(1)}, bf16[384,256]{1,0:T(8,128)(2,1)S(1)}, u32[]{:S(2)}, u32[]{:S(2)}) collective-permute-start(bf16[384,256]{1,0:T(8,128)(2,1)S(1)} %get-tuple-element.30.refs_0_), channel_id=1, source_target_pairs={{0,1},{1,2},{2,3},{3,4},{4,5},{5,6},{6,7},{7,0},{8,9},{9,10},{10,1... | collective-permute-start | bytes 589832 | tf_op jit(solution)/shard_map/ppermute | solution.py:473
  24.5 22.1 %collective-permute-start.4 = (bf16[384,256]{1,0:T(8,128)(2,1)S(1)}, bf16[384,256]{1,0:T(8,128)(2,1)S(1)}, u32[]{:S(2)}, u32[]{:S(2)}) collective-permute-start(bf16[384,256]{1,0:T(8,128)(2,1)S(1)} %get-tuple-element.29.refs_1_), channel_id=1, source_target_pairs={{0,1},{1,2},{2,3},{3,4},{4,5},{5,6},{6,7},{7,0},{8,9},{9,10},{10,1... | collective-permute-start | bytes 589832 | tf_op jit(solution)/shard_map/ppermute | solution.py:473
  24.5 22.2 %collective-permute-start.7 = (bf16[384,256]{1,0:T(8,128)(2,1)S(1)}, bf16[384,256]{1,0:T(8,128)(2,1)S(1)}, u32[]{:S(2)}, u32[]{:S(2)}) collective-permute-start(bf16[384,256]{1,0:T(8,128)(2,1)S(1)} %get-tuple-element.30.refs_0_), channel_id=1, source_target_pairs={{0,7},{1,0},{2,1},{3,2},{4,3},{5,4},{6,5},{7,6},{8,15},{9,8},{10,9... | collective-permute-start | bytes 589832 | tf_op jit(solution)/shard_map/ppermute | solution.py:474
  46.6 6.8 %collective-permute-start.2 = (bf16[384,256]{1,0:T(8,128)(2,1)S(1)}, bf16[384,256]{1,0:T(8,128)(2,1)S(1)}, u32[]{:S(2)}, u32[]{:S(2)}) collective-permute-start(bf16[384,256]{1,0:T(8,128)(2,1)S(1)} %collective-permute-done.1.refs_2_), channel_id=1, source_target_pairs={{0,1},{1,2},{2,3},{3,4},{4,5},{5,6},{6,7},{7,0},{8,9},{9,10},{10,1... | collective-permute-start | bytes 589832 | tf_op jit(solution)/shard_map/ppermute | solution.py:473
  46.6 10.4 %collective-permute-start.5 = (bf16[384,256]{1,0:T(8,128)(2,1)S(1)}, bf16[384,256]{1,0:T(8,128)(2,1)S(1)}, u32[]{:S(2)}, u32[]{:S(2)}) collective-permute-start(bf16[384,256]{1,0:T(8,128)(2,1)S(1)} %collective-permute-done.4.refs_3_), channel_id=1, source_target_pairs={{0,1},{1,2},{2,3},{3,4},{4,5},{5,6},{6,7},{7,0},{8,9},{9,10},{10,1... | collective-permute-start | bytes 589832 | tf_op jit(solution)/shard_map/ppermute | solution.py:473
  46.7 10.3 %collective-permute-start.8 = (bf16[384,256]{1,0:T(8,128)(2,1)S(1)}, bf16[384,256]{1,0:T(8,128)(2,1)S(1)}, u32[]{:S(2)}, u32[]{:S(2)}) collective-permute-start(bf16[384,256]{1,0:T(8,128)(2,1)S(1)} %collective-permute-done.7.refs_4_), channel_id=1, source_target_pairs={{0,7},{1,0},{2,1},{3,2},{4,3},{5,4},{6,5},{7,6},{8,15},{9,8},{10,9... | collective-permute-start | bytes 589832 | tf_op jit(solution)/shard_map/ppermute | solution.py:474
  49.8 10.0 %collective-permute-start.12 = (bf16[384,256]{1,0:T(8,128)(2,1)S(1)}, bf16[384,256]{1,0:T(8,128)(2,1)S(1)}, u32[]{:S(2)}, u32[]{:S(2)}) collective-permute-start(bf16[384,256]{1,0:T(8,128)(2,1)S(1)} %collective-permute-done.11.refs_9_), channel_id=1, source_target_pairs={{0,7},{1,0},{2,1},{3,2},{4,3},{5,4},{6,5},{7,6},{8,15},{9,8},{10,9... | collective-permute-start | bytes 589832 | tf_op jit(solution)/shard_map/ppermute | solution.py:474
  53.4 8.2 %collective-permute-start.3 = (bf16[384,256]{1,0:T(8,128)(2,1)S(1)}, bf16[384,256]{1,0:T(8,128)(2,1)S(1)}, u32[]{:S(2)}, u32[]{:S(2)}) collective-permute-start(bf16[384,256]{1,0:T(8,128)(2,1)S(1)} %collective-permute-done.2.refs_6_), channel_id=1, source_target_pairs={{0,1},{1,2},{2,3},{3,4},{4,5},{5,6},{6,7},{7,0},{8,9},{9,10},{10,1... | collective-permute-start | bytes 589832 | tf_op jit(solution)/shard_map/ppermute | solution.py:473
  57.0 6.7 %collective-permute-start.6 = (bf16[384,256]{1,0:T(8,128)(2,1)S(1)}, bf16[384,256]{1,0:T(8,128)(2,1)S(1)}, u32[]{:S(2)}, u32[]{:S(2)}) collective-permute-start(bf16[384,256]{1,0:T(8,128)(2,1)S(1)} %collective-permute-done.5.refs_7_), channel_id=1, source_target_pairs={{0,1},{1,2},{2,3},{3,4},{4,5},{5,6},{6,7},{7,0},{8,9},{9,10},{10,1... | collective-permute-start | bytes 589832 | tf_op jit(solution)/shard_map/ppermute | solution.py:473
  57.1 6.7 %collective-permute-start.9 = (bf16[384,256]{1,0:T(8,128)(2,1)S(1)}, bf16[384,256]{1,0:T(8,128)(2,1)S(1)}, u32[]{:S(2)}, u32[]{:S(2)}) collective-permute-start(bf16[384,256]{1,0:T(8,128)(2,1)S(1)} %collective-permute-done.8.refs_8_), channel_id=1, source_target_pairs={{0,7},{1,0},{2,1},{3,2},{4,3},{5,4},{6,5},{7,6},{8,15},{9,8},{10,9... | collective-permute-start | bytes 589832 | tf_op jit(solution)/shard_map/ppermute | solution.py:474
  59.7 6.8 %collective-permute-start.14 = (bf16[384,256]{1,0:T(8,128)(2,1)S(1)}, bf16[384,256]{1,0:T(8,128)(2,1)S(1)}, u32[]{:S(2)}, u32[]{:S(2)}) collective-permute-start(bf16[384,256]{1,0:T(8,128)(2,1)S(1)} %collective-permute-done.12.refs_13_), channel_id=1, source_target_pairs={{0,7},{1,0},{2,1},{3,2},{4,3},{5,4},{6,5},{7,6},{8,15},{9,8},{10,9... | collective-permute-start | bytes 589832 | tf_op jit(solution)/shard_map/ppermute | solution.py:479
  61.6 8.1 %collective-permute-start.13 = (bf16[384,256]{1,0:T(8,128)(2,1)S(1)}, bf16[384,256]{1,0:T(8,128)(2,1)S(1)}, u32[]{:S(2)}, u32[]{:S(2)}) collective-permute-start(bf16[384,256]{1,0:T(8,128)(2,1)S(1)} %collective-permute-done.3.refs_10_), channel_id=1, source_target_pairs={{0,1},{1,2},{2,3},{3,4},{4,5},{5,6},{6,7},{7,0},{8,9},{9,10},{10,1... | collective-permute-start | bytes 589832 | tf_op jit(solution)/shard_map/ppermute | solution.py:477
  70.4 21.5 %collective-permute-start.16 = (bf16[256,2048]{1,0:T(8,128)(2,1)S(1)}, bf16[256,2048]{1,0:T(8,128)(2,1)}, u32[]{:S(2)}, u32[]{:S(2)}) collective-permute-start(bf16[256,2048]{1,0:T(8,128)(2,1)S(1)} %collective-permute-done.refs_2_), channel_id=1, source_target_pairs={{0,1},{1,2},{2,3},{3,4},{4,5},{5,6},{6,7},{7,0},{8,15},{9,8},{10,9... | collective-permute-start | bytes 3145736 | tf_op jit(solution)/shard_map/ppermute | solution.py:548
  91.9 14.2 %collective-permute-start.18 = (bf16[256,2048]{1,0:T(8,128)(2,1)}, bf16[256,2048]{1,0:T(8,128)(2,1)S(1)}, u32[]{:S(2)}, u32[]{:S(2)}) collective-permute-start(bf16[256,2048]{1,0:T(8,128)(2,1)} %collective-permute-done.16.refs_4_), channel_id=1, source_target_pairs={{0,1},{1,2},{2,3},{3,4},{4,5},{5,6},{6,7},{7,0},{8,15},{9,8},{10,9... | collective-permute-start | bytes 3145736 | tf_op jit(solution)/shard_map/ppermute | solution.py:548
  106.1 8.6 %collective-permute-start.20 = (bf16[128,2048]{1,0:T(8,128)(2,1)S(1)}, bf16[128,2048]{1,0:T(8,128)(2,1)}, u32[]{:S(2)}, u32[]{:S(2)}) collective-permute-start(bf16[128,2048]{1,0:T(8,128)(2,1)S(1)} %constant_dynamic-slice_fusion), channel_id=1, source_target_pairs={{0,1},{1,2},{2,3},{3,4},{4,5},{5,6},{6,7},{7,0},{8,15},{9,8},{10,9... | collective-permute-start | bytes 1572872 | tf_op jit(solution)/shard_map/ppermute | solution.py:548
  108.5 36.0 %collective-permute-start.15 = (bf16[256,2048]{1,0:T(8,128)(2,1)}, bf16[256,2048]{1,0:T(8,128)(2,1)}, u32[]{:S(2)}, u32[]{:S(2)}) collective-permute-start(bf16[256,2048]{1,0:T(8,128)(2,1)} %copy-done.4), channel_id=1, source_target_pairs={{0,8},{1,9},{2,10},{3,11},{4,12},{5,13},{6,14},{7,15},{8,0},{9,1},... | collective-permute-start | bytes 3145736 | tf_op jit(solution)/shard_map/ppermute | solution.py:548
  113.7 30.8 %collective-permute-start.17 = (bf16[256,2048]{1,0:T(8,128)(2,1)}, bf16[256,2048]{1,0:T(8,128)(2,1)}, u32[]{:S(2)}, u32[]{:S(2)}) collective-permute-start(bf16[256,2048]{1,0:T(8,128)(2,1)} %collective-permute-done.16.refs_4_), channel_id=1, source_target_pairs={{0,8},{1,9},{2,10},{3,11},{4,12},{5,13},{6,14},{7,15},{8,0},{9,1},... | collective-permute-start | bytes 3145736 | tf_op jit(solution)/shard_map/ppermute | solution.py:548
  113.8 30.8 %collective-permute-start.19 = (bf16[256,2048]{1,0:T(8,128)(2,1)S(1)}, bf16[256,2048]{1,0:T(8,128)(2,1)}, u32[]{:S(2)}, u32[]{:S(2)}) collective-permute-start(bf16[256,2048]{1,0:T(8,128)(2,1)S(1)} %collective-permute-done.18.refs_6_), channel_id=1, source_target_pairs={{0,8},{1,9},{2,10},{3,11},{4,12},{5,13},{6,14},{7,15},{8,0},{9,1},... | collective-permute-start | bytes 3145736 | tf_op jit(solution)/shard_map/ppermute | solution.py:548
  114.7 29.9 %collective-permute-start.21 = (bf16[128,2048]{1,0:T(8,128)(2,1)}, bf16[128,2048]{1,0:T(8,128)(2,1)}, u32[]{:S(2)}, u32[]{:S(2)}) collective-permute-start(bf16[128,2048]{1,0:T(8,128)(2,1)} %collective-permute-done.20.refs_8_), channel_id=1, source_target_pairs={{0,8},{1,9},{2,10},{3,11},{4,12},{5,13},{6,14},{7,15},{8,0},{9,1},... | collective-permute-start | bytes 1572872 | tf_op jit(solution)/shard_map/ppermute | solution.py:548
  140.6 19.2 %all-to-all-start.1 = ((bf16[8,96,256]{2,1,0:T(8,128)(2,1)}), bf16[8,96,256]{2,1,0:T(8,128)(2,1)S(1)}, u32[]{:S(2)}, u32[]{:S(2)}) async-start(bf16[8,96,256]{2,1,0:T(8,128)(2,1)} %bitcast.16), calls=%async_computation.1 | async-start | bytes 786432 | tf_op jit(solution)/shard_map/all_to_all | solution.py:581
  166.1 18.5 %all-to-all-start.2 = ((bf16[8,96,256]{2,1,0:T(8,128)(2,1)}), bf16[8,96,256]{2,1,0:T(8,128)(2,1)S(1)}, u32[]{:S(2)}, u32[]{:S(2)}) async-start(bf16[8,96,256]{2,1,0:T(8,128)(2,1)} %bitcast.13), calls=%async_computation.2 | async-start | bytes 786432 | tf_op jit(solution)/shard_map/all_to_all | solution.py:592
  (24 other events, 433.4 us)
